TPU v7x, 256 devices: a whole 4x4x8 slice. The times are simulated.
256 devices in a mesh: tile: 32 (over y, z), curve: 8 (over x, core).
Axes of the slice: x: 4, y: 4, z: 8, core: 2. Of those that a mesh axis runs over, the one named last changes fastest.
Arguments:
- points: bfloat16 [32, 1024, 512], P('tile', 'curve'), may hold values from -6 to 6
- valid_rows: int32 [32, 8], P('tile', 'curve'), may hold values from 32 to 128, as said below
- dest_shard: int32 [32, 8, 1], P('tile', 'curve'), may hold values from 0 to 7, as said below
- dest_slot: int32 [32, 8, 1], P('tile', 'curve'), may hold values from 0 to 0, as said below
- norm_gain: float32 [2, 512], replicated, may hold values from 0.1 to 1.9
- w_xz: bfloat16 [2, 512, 2048], replicated, may hold values from -0.25 to 0.25
- w_bc: bfloat16 [2, 512, 256], replicated, may hold values from -0.25 to 0.25
- w_dt: bfloat16 [2, 512, 16], replicated, may hold values from -0.25 to 0.25
- dt_bias: float32 [2, 16], replicated, may hold values from -1 to 1
- decay_rate: float32 [2, 16], replicated, may hold values from 9.155273e-07 to 0.1
- skip_gain: float32 [2, 16], replicated, may hold values from 0.5 to 1.5
- gate_gain: float32 [2, 1024], replicated, may hold values from 0.1 to 1.9
- w_out: bfloat16 [2, 1024, 512], replicated, may hold values from -0.1875 to 0.1875
Outputs:
- mixed: bfloat16 [32, 1024, 512], P('tile', 'curve')
Inputs may be any that keep to these rules, and one draw needn't show every extreme that they name: `valid_rows`: every tile has a curve shard with all 128 points live. `dest_shard`: within each tile, the 1 block of a curve shard go to 1 different curve shards, and every curve shard receives 1 block, one for each slot. `dest_slot`: together with dest_shard, every slot of every curve shard is filled exactly once.
All inputs are finite; a program needn't handle non-finite values.
Results may differ from a plain program's by a relative error of at most 0.0061.
Values may be sent and summed in bfloat16 or wider, within the bound.
A program may use at most 320 MiB of HBM per device.

v0:
```python
import jax
import jax.numpy as jnp
from jax import lax
from jax.sharding import PartitionSpec as P

BLOCK = 128


highest = lax.Precision.HIGHEST


def carried_in(shard, axis, combine, identity):
    peers, place = (lax.axis_size(axis), lax.axis_index(axis))
    everything = jax.tree.map(lambda part: lax.all_gather(part, axis), shard)
    start = jax.tree.map(
        lambda part, zero: jnp.broadcast_to(jnp.asarray(zero, part.dtype), part.shape),
        shard,
        identity,
    )

    def lap(k, before):
        reached = k < place
        new = combine(before, jax.tree.map(lambda part: part[k], everything))
        return jax.tree.map(lambda a, b: jnp.where(reached, a, b), new, before)

    return lax.fori_loop(0, peers, lap, start)


def prepare(inputs, live_rows, norm_g, proj_xz, proj_bc, proj_dt, shift_dt, rate_dt):
    widened = inputs.astype(jnp.float32)
    scaled = (
        widened * lax.rsqrt(jnp.mean(widened * widened, axis=-1, keepdims=True) + 1e-05) * norm_g
    )
    normed = scaled.astype(jnp.bfloat16)
    joined = jnp.dot(normed, proj_xz, preferred_element_type=jnp.float32)
    inner_width = joined.shape[1] // 2
    values = jax.nn.silu(joined[:, :inner_width]).astype(jnp.bfloat16)
    gate_pre = joined[:, inner_width:]
    mixed_bc = jnp.dot(normed, proj_bc, preferred_element_type=jnp.float32)
    state_width = mixed_bc.shape[1] // 2
    key_rows = jax.nn.silu(mixed_bc[:, :state_width]).astype(jnp.bfloat16)
    query_rows = jax.nn.silu(mixed_bc[:, state_width:]).astype(jnp.bfloat16)
    step_sizes = (
        jax.nn.softplus(jnp.dot(normed, proj_dt, preferred_element_type=jnp.float32) + shift_dt)
        * live_rows[:, None]
    )
    running = jnp.cumsum(-step_sizes * rate_dt, axis=0)
    log_total = running[-1]
    head_count = step_sizes.shape[1]
    head_values = values.astype(jnp.float32).reshape(values.shape[0], head_count, -1)
    to_end = jnp.exp(log_total[None, :] - running) * step_sizes
    end_state = jnp.einsum(
        "shp,sn->hpn",
        head_values * to_end[:, :, None],
        key_rows.astype(jnp.float32),
        precision=highest,
    )
    return (
        (log_total, end_state),
        (widened, gate_pre, key_rows, query_rows, step_sizes, running, head_values),
    )


def finish(carried, pieces, skip_g, gate_g, proj_out, live_rows):
    widened, gate_pre, key_rows, query_rows, step_sizes, running, head_values = pieces
    row_count = widened.shape[0]
    block_rows = min(512, row_count)
    running_heads = running.T
    steps_heads = step_sizes.T
    scores = jnp.dot(query_rows, key_rows.T, preferred_element_type=jnp.float32)
    causal = (0 + lax.iota(jnp.int32, block_rows))[:, None] >= lax.iota(jnp.int32, block_rows)[
        None, :
    ]
    gaps = running_heads[:, 0:block_rows, None] - running_heads[:, None, :block_rows]
    weights = jnp.where(causal[None], jnp.exp(jnp.where(causal[None], gaps, 0.0)), 0.0)
    weights = weights * steps_heads[:, None, :block_rows] * scores[None]
    inside = jnp.einsum("hts,shp->thp", weights, head_values, precision=highest)
    from_state = jnp.einsum(
        "hpn,tn->thp", carried, query_rows.astype(jnp.float32), precision=highest
    )
    carried_part = jnp.exp(running)[:, :, None] * from_state
    outputs = inside + carried_part + skip_g[None, :, None] * head_values
    head_out = outputs.reshape(row_count, -1)
    gated = head_out * jax.nn.silu(gate_pre)
    normed = (
        gated * lax.rsqrt(jnp.mean(gated * gated, axis=-1, keepdims=True) + 1e-05) * gate_g
    ).astype(jnp.bfloat16)
    update = jnp.dot(normed, proj_out, preferred_element_type=jnp.float32)
    return (widened + live_rows[:, None] * update).astype(jnp.bfloat16)


def chain_combine(earlier, later):
    return (earlier[0] + later[0], jnp.exp(later[0])[:, None, None] * earlier[1] + later[1])


def local(
    points,
    valid_rows,
    dest_shard,
    dest_slot,
    norm_gain,
    w_xz,
    w_bc,
    w_dt,
    dt_bias,
    decay_rate,
    skip_gain,
    gate_gain,
    w_out,
):
    inputs = points[0]
    row_count = inputs.shape[0]
    model_width = inputs.shape[1]
    row_index = lax.iota(jnp.int32, row_count)
    live_first = (row_index < valid_rows[0, 0]).astype(jnp.float32)
    summary, pieces = prepare(
        inputs, live_first, norm_gain[0], w_xz[0], w_bc[0], w_dt[0], dt_bias[0], decay_rate[0]
    )
    identity_pair = (jnp.zeros_like(summary[0]), jnp.zeros_like(summary[1]))
    incoming = carried_in(summary, "curve", chain_combine, identity_pair)
    first_out = finish(incoming[1], pieces, skip_gain[0], gate_gain[0], w_out[0], live_first)
    curves = lax.axis_size("curve")
    block_count = row_count // BLOCK
    targets = dest_shard[0, 0]
    slot_ids = dest_slot[0, 0]
    block_live = jnp.clip(valid_rows[0, 0] - lax.iota(jnp.int32, block_count) * BLOCK, 0, BLOCK)
    outgoing = lax.iota(jnp.int32, curves)[:, None] == targets[None, :]
    send_rows = jnp.dot(
        outgoing.astype(jnp.bfloat16),
        first_out.reshape(block_count, -1),
        preferred_element_type=jnp.float32,
    )
    send_rows = send_rows.astype(jnp.bfloat16).reshape(curves, BLOCK, model_width)
    send_slots = jnp.sum(jnp.where(outgoing, slot_ids[None, :] + 1, 0), axis=1) - 1
    send_live = jnp.sum(jnp.where(outgoing, block_live[None, :], 0), axis=1)
    got_rows, got_slots, got_live = (
        lax.all_to_all(send_rows, "curve", split_axis=0, concat_axis=0, tiled=True),
        lax.all_to_all(send_slots, "curve", split_axis=0, concat_axis=0, tiled=True),
        lax.all_to_all(send_live, "curve", split_axis=0, concat_axis=0, tiled=True),
    )
    placing = lax.iota(jnp.int32, block_count)[:, None] == got_slots[None, :]
    second_in = jnp.dot(
        placing.astype(jnp.bfloat16),
        got_rows.reshape(curves, -1),
        preferred_element_type=jnp.float32,
    )
    second_in = second_in.astype(jnp.bfloat16).reshape(row_count, model_width)
    placed_live = jnp.sum(jnp.where(placing, got_live[None, :], 0), axis=1)
    live_second = (
        (lax.iota(jnp.int32, BLOCK)[None, :] < placed_live[:, None])
        .reshape(row_count)
        .astype(jnp.float32)
    )
    summary_two, pieces_two = prepare(
        second_in, live_second, norm_gain[1], w_xz[1], w_bc[1], w_dt[1], dt_bias[1], decay_rate[1]
    )
    incoming_two = carried_in(summary_two, ("tile", "curve"), chain_combine, identity_pair)
    second_out = finish(
        incoming_two[1], pieces_two, skip_gain[1], gate_gain[1], w_out[1], live_second
    )
    return second_out[None]


def solution(mesh):
    in_specs = (
        P("tile", "curve", None),
        P("tile", "curve"),
        P("tile", "curve", None),
        P("tile", "curve", None),
        P(),
        P(),
        P(),
        P(),
        P(),
        P(),
        P(),
        P(),
        P(),
    )
    out_specs = P("tile", "curve", None)
    return jax.shard_map(local, mesh=mesh, in_specs=in_specs, out_specs=out_specs, check_vma=False)
```

profile of v0, /device:TPU:1, one launch (start us, length us, event | category | flops | bytes accessed | tf_op | source)
XLA Modules:
  0.0 770.0 jit_solution(17066219720648469685)
XLA Ops:
  11.3 2.2 fusion.4
  14.2 1.2 fusion.35
  17.3 6.4 all-to-all-start
  23.9 10.9 %all-gather.2 = f32[8,1,16]{2,1,0:T(1,128)S(1)} all-gather(f32[1,1,16]{2,1,0:T(1,128)S(1)} %get-tuple-element.254), channel_id=1, replica_groups=mesh['tile'=32,'curve'=8] {'curve'}, dimensions={0}, use_global_device_ids=true | all-gather | bytes 576 | tf_op jit(solution)/shard_map/all_gather | solution.py:14
  35.0 19.3 %all-gather.7.cloned.1.call-done = f32[128,64,128]{2,1,0:T(8,128)} async-done(((f32[16,64,128]{2,1,0:T(8,128)}), f32[128,64,128]{2,1,0:T(8,128)}) %all-gather.7.cloned.1.call-update) | async-done | bytes 4194320 | tf_op jit(solution)/shard_map/all_gather | solution.py:14
  54.3 9.7 %while.28 = (s32[]{:T(128)}, f32[16,64,128]{2,1,0:T(8,128)S(1)}, s32[]{:T(128)}, f32[8,16]{1,0:T(8,128)S(1)}, f32[8,16,64,128]{3,2,1,0:T(8,128)}, /*index=5*/s32[]{:T(128)}, s32[]{:T(128)}) while((s32[]{:T(128)}, f32[16,64,128]{2,1,0:T(8,128)S(1)}, s32[]{:T(128)}, f32[8,16]{1,0:T(8,128)S(1)}, f32[8,16,64,128]{3,2,1,0:T(8,128)}, ...), condition=%wide.region_3.4_spmd.clone, body=%wide.region_2.3_spmd.clone.sunk | while | flops 524292 | bytes 1573161 | solution.py:26
  54.4 1.2 fusion.110
  55.6 1.2 fusion.110
  56.8 1.2 fusion.110
  60.4 1.2 fusion.110
  64.4 1.3 fusion.11
  66.2 1.6 fusion.16
  68.1 1.3 copy.78
  69.4 7.6 all_to_all.17
  77.0 4.2 all-to-all-start.1
  82.8 13.4 %all-to-all-done.1 = bf16[8,128,512]{2,1,0:T(8,128)(2,1)S(1)} async-done(((bf16[8,128,512]{2,1,0:T(8,128)(2,1)}), bf16[8,128,512]{2,1,0:T(8,128)(2,1)S(1)}, u32[]{:S(2)}, u32[]{:S(2)}) %all-to-all-start.1) | async-done | bytes 1048608 | tf_op jit(solution)/shard_map/all_to_all | solution.py:137
  98.2 2.1 fusion.2
  100.9 1.2 fusion.36
  102.3 57.9 %all-gather.3 = f32[256,1,16]{2,1,0:T(1,128)S(1)} all-gather(f32[1,1,16]{2,1,0:T(1,128)S(1)} %get-tuple-element.252), channel_id=1, replica_groups=mesh['tile'=32,'curve'=8] {'tile','curve'}, dimensions={0}, use_global_device_ids=true | all-gather | bytes 16448 | tf_op jit(solution)/shard_map/all_gather | solution.py:14
  160.3 287.3 %all-gather.9.cloned.1.call-done = f32[4096,64,128]{2,1,0:T(8,128)} async-done(((f32[16,64,128]{2,1,0:T(8,128)}), f32[4096,64,128]{2,1,0:T(8,128)}) %all-gather.9.cloned.1.call-update) | async-done | bytes 134217744 | tf_op jit(solution)/shard_map/all_gather | solution.py:14
  447.6 311.1 %while.29 = (s32[]{:T(128)}, f32[16,64,128]{2,1,0:T(8,128)S(1)}, s32[]{:T(128)}, f32[256,16]{1,0:T(8,128)S(1)}, f32[256,16,64,128]{3,2,1,0:T(8,128)}, /*index=5*/s32[]{:T(128)}, s32[]{:T(128)}) while((s32[]{:T(128)}, f32[16,64,128]{2,1,0:T(8,128)S(1)}, s32[]{:T(128)}, f32[256,16]{1,0:T(8,128)S(1)}, ...), condition=%wide.region_9.10_spmd.clone, body=%wide.region_8.9_spmd.clone.sunk | while | flops 524292 | bytes 1573161 | solution.py:26
  447.6 1.2 fusion.111
  759.1 1.3 fusion.9
  760.9 2.3 fusion.18
  (604 shorter events, 318.8 us)
Async XLA Ops:
  6.5 47.8 %all-gather.7.cloned.1.call-start = ((), (), s32[]{:S(2)}) async-start(), calls=%async_computation.3 | async-start | bytes 4718592 | tf_op jit(solution)/shard_map/all_gather | solution.py:14
  11.2 2.6 copy-start
  11.3 2.6 copy-start.1
  13.5 21.3 %copy-start.3 = (f32[2,16]{1,0:T(2,128)S(1)}, f32[2,16]{1,0:T(2,128)}, u32[]{:S(2)}) copy-start(f32[2,16]{1,0:T(2,128)} %param.27) | copy-start | bytes 388
  13.5 21.3 %copy-start.2 = (f32[2,1024]{1,0:T(2,128)S(1)}, f32[2,1024]{1,0:T(2,128)}, u32[]{:S(2)}) copy-start(f32[2,1024]{1,0:T(2,128)} %param.28) | copy-start | bytes 24580
  17.3 52.1 %all-to-all-start = ((s32[8,1,1]{2,1,0:T(1,128)}), s32[8,1,1]{2,1,0:T(1,128)S(1)}, u32[]{:S(2)}, u32[]{:S(2)}) async-start(s32[8,1,1]{2,1,0:T(1,128)} %fusion.86), calls=%async_computation | async-start | bytes 8192 | tf_op jit(solution)/shard_map/all_to_all | solution.py:138
  77.0 19.2 %all-to-all-start.1 = ((bf16[8,128,512]{2,1,0:T(8,128)(2,1)}), bf16[8,128,512]{2,1,0:T(8,128)(2,1)S(1)}, u32[]{:S(2)}, u32[]{:S(2)}) async-start(bf16[8,128,512]{2,1,0:T(8,128)(2,1)} %bitcast.179), calls=%async_computation.1 | async-start | bytes 2097152 | tf_op jit(solution)/shard_map/all_to_all | solution.py:137
  81.2 366.5 %all-gather.9.cloned.1.call-start = ((), (), s32[]{:S(2)}) async-start(), calls=%async_computation.4 | async-start | bytes 134742016 | tf_op jit(solution)/shard_map/all_gather | solution.py:14
  96.7 1.0 copy-start.4
Sparse Core Ops, SparseCore 0:
  15.5 38.7 all-gather.6
  102.2 345.3 all-gather.8
where the time goes:
time: 783 us; the launch traced here: 770 us
  waiting for transfers between devices  320 us (41%)
  other arithmetic  314 us (40%)
  blocking collectives  76.4 us (10%)
  matrix products  16.5 us (2%)
  between operations  15.7 us (2%)
  starting transfers between devices  10.6 us (1%)
  local copies, waits for them, and re-layouts  8.24 us (1%)
  loops' own time  8.15 us (1%)
    select_n x264, other arithmetic, lap(): return jax.tree.map(lambda a, b: jnp.where(reached, a, b), new, before)  310 us
    all_gather x2, waiting for transfers between devices, carried_in(): everything = jax.tree.map(lambda part: lax.all_gather(part, axis), shard)  307 us
    all_gather x2, blocking collectives, carried_in(): everything = jax.tree.map(lambda part: lax.all_gather(part, axis), shard)  68.8 us
  transfers between devices with their start and end apart: 4, of which 3 were waited for; matrix products, arithmetic and copies ran while one was open for 2% of the time, Pallas kernels for 0%

commit v1 on v0

v1 whole, which is shorter than its diff:
```python
import functools

import jax
import jax.numpy as jnp
from jax import lax
from jax.experimental import pallas as pl
from jax.experimental.pallas import tpu as pltpu
from jax.sharding import PartitionSpec as P

F32 = jnp.float32
BF16 = jnp.bfloat16
HI = lax.Precision.HIGHEST
NC = 8
R = 128
D = 512
E = 1024
H = 16
CH = 512


def silu(v):
    return v * jax.nn.sigmoid(v)


def softplus(v):
    return jnp.maximum(v, 0.0) + jnp.log1p(jnp.exp(-jnp.abs(v)))


def mesh_copy(src, dst, send_sem, recv_sem, tile, curve):
    return pltpu.make_async_remote_copy(
        src_ref=src,
        dst_ref=dst,
        send_sem=send_sem,
        recv_sem=recv_sem,
        device_id=(tile, curve),
        device_id_type=pl.DeviceIdType.MESH,
    )


def kernel(
    NY,
    NZ,
    valid_s,
    dest_s,
    x_h,
    ng_h,
    wxz_h,
    wbc_h,
    wdt_h,
    dtb_h,
    rate_h,
    skip_h,
    gg_h,
    wout_h,
    out_h,
    x_v,
    ng,
    wxz,
    wbc,
    wdt,
    dtb,
    rate,
    skip,
    gg,
    wout,
    in_sem,
    exp_m,
    vals,
    gate,
    inner,
    decx,
    sA,
    rA,
    lS,
    lR,
    sC,
    rC,
    pre,
    lpre,
    sB1,
    rB1,
    sB2,
    rB2,
    sB3,
    rB3,
    mS,
    mR,
    pS,
    pR,
    out_v,
    a_send,
    a_recv,
    l_send,
    l_recv,
    c_send,
    c_recv,
    b1_send,
    b1_recv,
    b2_send,
    b2_recv,
    b3_send,
    b3_recv,
    m_send,
    m_recv,
    out_sem,
):
    t = lax.axis_index("tile")
    c = lax.axis_index("curve")
    y = t // NZ
    z = lax.rem(t, NZ)
    RZ = R // NZ
    curve_peer = [lax.rem(c + k, NC) for k in range(NC)]
    z_peer = [lax.rem(z + k, NZ) for k in range(NZ)]
    y_peer = [lax.rem(y + k, NY) for k in range(NY)]

    barrier = pltpu.get_barrier_semaphore()

    def hello(tile, curve):
        pl.semaphore_signal(
            barrier, inc=1, device_id=(tile, curve), device_id_type=pl.DeviceIdType.MESH
        )

    for k in range(1, NC):
        hello(t, curve_peer[k])
    for k in range(1, NZ):
        hello(y * NZ + z_peer[k], c)
    for k in range(1, NY):
        hello(y_peer[k] * NZ + z, c)

    n_in = [0]

    def fetch(src, dst):
        cp = pltpu.make_async_copy(src, dst, in_sem.at[n_in[0]])
        n_in[0] += 1
        cp.start()
        return cp

    x_cp = fetch(x_h.at[0], x_v)
    small_cp = [
        fetch(a, b)
        for a, b in ((ng_h, ng), (dtb_h, dtb), (rate_h, rate), (skip_h, skip), (gg_h, gg))
    ]
    dt_cp = [fetch(wdt_h.at[0], wdt.at[0])]
    bc_cp = [fetch(wbc_h.at[0], wbc.at[0])]

    def fetch_xz(layer):
        return [
            fetch(wxz_h.at[layer, :, pl.ds(q * CH, CH)], wxz.at[layer, q])
            for q in range(2 * E // CH)
        ]

    xz_cp = [fetch_xz(0)]
    out_cp = [fetch(wout_h.at[0], wout.at[0])]

    lane = lax.broadcasted_iota(jnp.int32, (R, R), 1)
    row = lax.broadcasted_iota(jnp.int32, (R, R), 0)
    row_f = row.astype(F32)
    causal = row >= lane
    tri = jnp.where(causal, 1.0, 0.0).astype(F32)
    erow = lax.broadcasted_iota(jnp.int32, (R, E), 0)
    ecol = lax.broadcasted_iota(jnp.int32, (R, E), 1)
    exp_m[...] = jnp.where(
        jnp.logical_and(erow < 48, (erow & 15) == (ecol >> 6)), 1.0, 0.0
    ).astype(BF16)
    rep = jnp.where(
        lax.broadcasted_iota(jnp.int32, (H, R), 0)
        == (lax.broadcasted_iota(jnp.int32, (H, R), 1) & 15),
        1.0,
        0.0,
    )
    rep_b = rep.astype(BF16)

    def widen(v):
        hi = v.astype(BF16).astype(F32)
        rest = v - hi
        mid = rest.astype(BF16).astype(F32)
        low = rest - mid
        ln = lax.broadcasted_iota(jnp.int32, v.shape, 1)
        parts = jnp.where(ln < 16, hi, jnp.where(ln < 32, mid, low)).astype(BF16)
        return jnp.dot(parts, exp_m[...], preferred_element_type=F32)

    def copies8(v):
        return jnp.dot(v, rep, precision=HI, preferred_element_type=F32)

    x_cp.wait()
    for cp in small_cp:
        cp.wait()
    bias8, rate8, skip8 = copies8(dtb[...]), copies8(rate[...]), copies8(skip[...])
    skip_x = widen(jnp.concatenate([skip8] * 4, axis=0))

    valid_row = jnp.full((1, R), valid_s[0, 0], jnp.int32).astype(F32)
    dest_row = jnp.full((1, R), dest_s[0, 0, 0], jnp.int32).astype(F32)

    def norm_of(xb, layer):
        w = xb.astype(F32)
        ms = jnp.mean(w * w, axis=-1, keepdims=True)
        return (w * lax.rsqrt(ms + 1e-05) * ng[layer : layer + 1, :]).astype(BF16)

    def times_of(nb, live, layer):
        wrep = jnp.dot(wdt[layer], rep_b, preferred_element_type=F32).astype(BF16)
        steps = softplus(
            jnp.dot(nb, wrep, preferred_element_type=F32) + bias8[layer : layer + 1, :]
        )
        steps = steps * live
        running = jnp.dot(
            tri, -steps * rate8[layer : layer + 1, :], precision=HI, preferred_element_type=F32
        )
        return steps, running

    def project_values(nb, layer):
        for q in range(E // CH):
            v = jnp.dot(nb, wxz[layer, q], preferred_element_type=F32)
            vals[:, q * CH : (q + 1) * CH] = silu(v).astype(BF16)

    def project_gate(nb, layer):
        for q in range(E // CH):
            v = jnp.dot(nb, wxz[layer, q + E // CH], preferred_element_type=F32)
            gate[:, q * CH : (q + 1) * CH] = silu(v)

    def keys_of(nb, layer):
        return silu(jnp.dot(nb, wbc[layer, :, 0:R], preferred_element_type=F32))

    def queries_of(nb, layer):
        return silu(jnp.dot(nb, wbc[layer, :, R : 2 * R], preferred_element_type=F32)).astype(BF16)

    def summary(layer, steps, running, keys):
        total = running[R - 1 : R, :]
        wide = widen(jnp.exp(total - running) * steps)
        keys_t = keys.T.astype(BF16)
        for j in range(NC):
            cols = slice(j * R, (j + 1) * R)
            scaled = (vals[:, cols].astype(F32) * wide[:, cols]).astype(BF16)
            sA[layer, j] = jnp.dot(keys_t, scaled, preferred_element_type=F32).astype(BF16)
        total_x = widen(jnp.broadcast_to(total, (8, R)))
        for j in range(NC):
            lS[layer, j : j + 1, :] = total_x[0:1, j * R : (j + 1) * R]
        if layer == 0:
            lS[layer, 8:16, :] = jnp.concatenate(
                [dest_row, valid_row, jnp.zeros((6, R), F32)], axis=0
            )
        else:
            lS[layer, 8:16, :] = jnp.zeros((8, R), F32)

    sent = []

    def send_summary(layer):
        got = []
        for k in range(1, NC):
            cp = mesh_copy(
                lS.at[layer],
                lR.at[layer, c],
                l_send.at[layer, k],
                l_recv.at[layer, k],
                t,
                curve_peer[k],
            )
            cp.start()
            got.append(cp)
            cp = mesh_copy(
                sA.at[layer, curve_peer[k]],
                rA.at[layer, c],
                a_send.at[layer, k],
                a_recv.at[layer, k],
                t,
                curve_peer[k],
            )
            cp.start()
            got.append(cp)
        lR[layer, c] = lS[layer]
        rA[layer, c] = sA[layer, c]
        sent.extend(got)
        return got

    def arrive(copies):
        for cp in copies:
            cp.wait_recv()

    def chain(layer):
        logs = [lR[layer, s, pl.ds(c, 1), :] for s in range(NC)]
        if layer == 0:
            place = [jnp.full((1, R), float(s), F32) for s in range(NC)]
        else:
            place = [lR[0, s, 8:9, :] for s in range(NC)]

        def lap(p, carry):
            state, log_sum = carry
            if layer == 0:
                sC[0, p] = state.astype(BF16)
            else:
                pre[p] = state
                lpre[p] = jnp.broadcast_to(log_sum, (8, R))
            pf = p.astype(F32)
            here = [jnp.where(place[s] == pf, 1.0, 0.0) for s in range(NC)]
            log_p = here[0] * logs[0]
            new = here[0] * rA[layer, 0].astype(F32)
            for s in range(1, NC):
                log_p = log_p + here[s] * logs[s]
                new = new + here[s] * rA[layer, s].astype(F32)
            return jnp.exp(log_p) * state + new, log_sum + log_p

        return lax.fori_loop(0, NC, lap, (jnp.zeros((R, R), F32), jnp.zeros((1, R), F32)))

    def send_carried(layer):
        got = []
        for k in range(1, NC):
            cp = mesh_copy(
                sC.at[layer, curve_peer[k]],
                rC.at[layer, c],
                c_send.at[layer, k],
                c_recv.at[layer, k],
                t,
                curve_peer[k],
            )
            cp.start()
            got.append(cp)
        rC[layer, c] = sC[layer, c]
        sent.extend(got)
        return got

    def inside(layer, steps, running, keys, queries):
        scores = lax.dot_general(
            queries, keys.astype(BF16), (((1,), (1,)), ((), ())), preferred_element_type=F32
        )
        scores = jnp.where(causal, scores, 0.0)
        running_t = running.T
        steps_t = steps.T
        half = lane < 64
        decx[...] = widen(jnp.exp(running))

        for j in range(NC):
            cols = slice(j * R, (j + 1) * R)
            v = vals[:, cols]
            vf = v.astype(F32)
            acc = skip_x[layer : layer + 1, cols] * vf
            for e in range(2):
                h = 2 * j + e
                gap = running[:, h : h + 1] - running_t[h : h + 1, :]
                w = jnp.exp(jnp.minimum(gap, 0.0)) * steps_t[h : h + 1, :] * scores
                ve = jnp.where(half if e == 0 else jnp.logical_not(half), vf, 0.0)
                acc = acc + jnp.dot(w.astype(BF16), ve.astype(BF16), preferred_element_type=F32)
            inner[:, cols] = acc

    def finish(layer, xb, live_col, queries):
        squares = jnp.zeros((R, R), F32)
        for j in range(NC):
            cols = slice(j * R, (j + 1) * R)
            from_state = jnp.dot(queries, rC[layer, j], preferred_element_type=F32)
            g = (inner[:, cols] + decx[:, cols] * from_state) * gate[:, cols]
            squares = squares + g * g
            inner[:, cols] = g
        scale = lax.rsqrt(jnp.sum(squares, axis=-1, keepdims=True) * (1.0 / E) + 1e-05)
        scaled = (inner[...] * scale * gg[layer : layer + 1, :]).astype(BF16)
        update = jnp.dot(scaled, wout[layer], preferred_element_type=F32)
        return (xb.astype(F32) + live_col * update).astype(BF16)

    xb = x_v[...]
    live = jnp.where(row_f < valid_row, 1.0, 0.0)
    nb = norm_of(xb, 0)
    dt_cp[0].wait()
    steps, running = times_of(nb, live, 0)
    bc_cp[0].wait()
    keys = keys_of(nb, 0)
    xz_cp[0][0].wait()
    xz_cp[0][1].wait()
    project_values(nb, 0)
    summary(0, steps, running, keys)
    pl.semaphore_wait(barrier, (NC - 1) + (NZ - 1) + (NY - 1))
    got = send_summary(0)
    dt_cp.append(fetch(wdt_h.at[1], wdt.at[1]))
    bc_cp.append(fetch(wbc_h.at[1], wbc.at[1]))
    xz_cp.append(fetch_xz(1))
    out_cp.append(fetch(wout_h.at[1], wout.at[1]))
    xz_cp[0][2].wait()
    xz_cp[0][3].wait()
    project_gate(nb, 0)
    queries = queries_of(nb, 0)
    arrive(got)
    chain(0)
    got = send_carried(0)
    inside(0, steps, running, keys, queries)
    out_cp[0].wait()
    arrive(got)
    first = finish(0, xb, live[:, 0:1], queries)
    mS[...] = first

    nb = norm_of(first, 1)
    dt_cp[1].wait()
    steps, running = times_of(nb, live, 1)
    bc_cp[1].wait()
    keys = keys_of(nb, 1)
    for cp in xz_cp[1]:
        cp.wait()
    out_cp[1].wait()
    project_values(nb, 1)
    summary(1, steps, running, keys)
    got_a = send_summary(1)

    got_m = []
    for k in range(1, 4):
        cp = mesh_copy(
            mS, mR.at[k], m_send.at[k], m_recv.at[k], t, lax.rem(c + 2 * k, NC)
        )
        cp.start()
        got_m.append(cp)
    sent.extend(got_m)

    arrive(got_a)
    tile_state, tile_log = chain(1)
    for k in range(NZ):
        sB1[k, 0:RZ, :] = tile_state[k * RZ : (k + 1) * RZ, :]
        sB1[k, RZ : RZ + 8, :] = jnp.broadcast_to(tile_log, (8, R))
    got = []
    for k in range(1, NZ):
        cp = mesh_copy(
            sB1.at[z_peer[k]],
            rB1.at[z],
            b1_send.at[k],
            b1_recv.at[k],
            y * NZ + z_peer[k],
            c,
        )
        cp.start()
        got.append(cp)
    rB1[z] = sB1[z]
    sent.extend(got)
    arrive(got)

    state = jnp.zeros((RZ, R), F32)
    log_sum = jnp.zeros((1, R), F32)
    row_states, row_logs = [], []
    for k in range(NZ):
        row_states.append(state)
        row_logs.append(log_sum)
        log_k = rB1[k, RZ : RZ + 1, :]
        state = jnp.exp(log_k) * state + rB1[k, 0:RZ, :]
        log_sum = log_sum + log_k
    sB2[0:RZ, :] = state
    sB2[RZ : RZ + 8, :] = jnp.broadcast_to(log_sum, (8, R))
    got = []
    for k in range(1, NY):
        cp = mesh_copy(
            sB2, rB2.at[y], b2_send.at[k], b2_recv.at[k], y_peer[k] * NZ + z, c
        )
        cp.start()
        got.append(cp)
    rB2[y] = sB2[...]
    sent.extend(got)

    arrive(got_m)
    partner = c + 1 - 2 * lax.rem(c, 2)
    c_f, partner_f = c.astype(F32), partner.astype(F32)
    mine = jnp.zeros((R, D), F32)
    theirs = jnp.zeros((R, D), F32)
    for k in range(4):
        src = lax.rem(c + NC - 2 * k, NC)
        goes = lR[0, src, 8:9, :]
        blk = (first if k == 0 else mR[k]).astype(F32)
        m_mine = jnp.concatenate([jnp.where(goes == c_f, 1.0, 0.0)] * 4, axis=1)
        m_theirs = jnp.concatenate([jnp.where(goes == partner_f, 1.0, 0.0)] * 4, axis=1)
        mine = mine + m_mine * blk
        theirs = theirs + m_theirs * blk
    pS[...] = theirs.astype(BF16)
    swap = mesh_copy(pS, pR, m_send.at[0], m_recv.at[0], t, partner)
    swap.start()
    sent.append(swap)
    valid_row = jnp.zeros((1, R), F32)
    for s in range(NC):
        valid_row = valid_row + jnp.where(lR[0, s, 8:9, :] == c_f, 1.0, 0.0) * lR[0, s, 9:10, :]
    live = jnp.where(row_f < valid_row, 1.0, 0.0)

    arrive(got)
    state = jnp.zeros((RZ, R), F32)
    for k in range(NY):
        new = jnp.exp(rB2[k, RZ : RZ + 1, :]) * state + rB2[k, 0:RZ, :]
        state = jnp.where(k < y, new, state)
    for k in range(NZ):
        sB3[k] = (jnp.exp(row_logs[k]) * state + row_states[k]).astype(BF16)
    got = []
    for k in range(1, NZ):
        cp = mesh_copy(
            sB3.at[z_peer[k]],
            rB3.at[z],
            b3_send.at[k],
            b3_recv.at[k],
            y * NZ + z_peer[k],
            c,
        )
        cp.start()
        got.append(cp)
    rB3[z] = sB3[z]
    sent.extend(got)

    swap.wait_recv()
    xb = (mine + pR[...].astype(F32)).astype(BF16)
    nb = norm_of(xb, 1)
    steps, running = times_of(nb, live, 1)
    keys = keys_of(nb, 1)
    queries = queries_of(nb, 1)
    project_values(nb, 1)

    arrive(got)
    entry = jnp.concatenate([rB3[k].astype(F32) for k in range(NZ)], axis=0)
    for p in range(NC):
        sC[1, p] = (jnp.exp(lpre[p, 0:1, :]) * entry + pre[p]).astype(BF16)
    got = send_carried(1)
    project_gate(nb, 1)
    inside(1, steps, running, keys, queries)
    arrive(got)
    out_v[...] = finish(1, xb, live[:, 0:1], queries)
    done = pltpu.make_async_copy(out_v, out_h.at[0], out_sem)
    done.start()
    for cp in sent:
        cp.wait_send()
    done.wait()


def call(NY, NZ, points, valid_rows, dest_shard, *params):
    RZ = R // NZ
    V = pltpu.VMEM
    DMA = pltpu.SemaphoreType.DMA
    any_spec = pl.BlockSpec(memory_space=pl.ANY)
    smem = pl.BlockSpec(memory_space=pltpu.SMEM)
    return pl.pallas_call(
        functools.partial(kernel, NY, NZ),
        out_shape=jax.ShapeDtypeStruct(points.shape, points.dtype),
        in_specs=[smem, smem] + [any_spec] * 10,
        out_specs=any_spec,
        scratch_shapes=[
            V((R, D), BF16),
            V((2, D), F32),
            V((2, 2 * E // CH, D, CH), BF16),
            V((2, D, 2 * R), BF16),
            V((2, D, H), BF16),
            V((2, H), F32),
            V((2, H), F32),
            V((2, H), F32),
            V((2, E), F32),
            V((2, E, D), BF16),
            DMA((20,)),
            V((R, E), BF16),
            V((R, E), BF16),
            V((R, E), F32),
            V((R, E), F32),
            V((R, E), F32),
            V((2, NC, R, R), BF16),
            V((2, NC, R, R), BF16),
            V((2, 16, R), F32),
            V((2, NC, 16, R), F32),
            V((2, NC, R, R), BF16),
            V((2, NC, R, R), BF16),
            V((NC, R, R), F32),
            V((NC, 8, R), F32),
            V((NZ, RZ + 8, R), F32),
            V((NZ, RZ + 8, R), F32),
            V((RZ + 8, R), F32),
            V((NY, RZ + 8, R), F32),
            V((NZ, RZ, R), BF16),
            V((NZ, RZ, R), BF16),
            V((R, D), BF16),
            V((4, R, D), BF16),
            V((R, D), BF16),
            V((R, D), BF16),
            V((R, D), BF16),
            DMA((2, NC)),
            DMA((2, NC)),
            DMA((2, NC)),
            DMA((2, NC)),
            DMA((2, NC)),
            DMA((2, NC)),
            DMA((NZ,)),
            DMA((NZ,)),
            DMA((NY,)),
            DMA((NY,)),
            DMA((NZ,)),
            DMA((NZ,)),
            DMA((4,)),
            DMA((4,)),
            DMA(()),
        ],
        compiler_params=pltpu.CompilerParams(
            collective_id=0, has_side_effects=True, vmem_limit_bytes=48 * 1024 * 1024
        ),
    )(valid_rows, dest_shard, points, *params)


def solution(mesh):
    tiles = mesh.shape["tile"]
    NZ = min(8, max(1, tiles // 2))
    NY = tiles // NZ

    def local(points, valid_rows, dest_shard, dest_slot, *params):
        return call(NY, NZ, points, valid_rows, dest_shard, *params)

    in_specs = (
        P("tile", "curve", None),
        P("tile", "curve"),
        P("tile", "curve", None),
        P("tile", "curve", None),
    ) + (P(),) * 9
    return jax.shard_map(
        local, mesh=mesh, in_specs=in_specs, out_specs=P("tile", "curve", None), check_vma=False
    )
```

time: 783 us -> 61.3 us (0.08); the launches traced: 770 us -> 60.9 us
  waiting for transfers between devices: 320 us -> 0 us
  other arithmetic: 314 us -> 0 us
  blocking collectives: 76.4 us -> 0 us
  Pallas kernels: 0 us -> 51 us
  matrix products: 16.5 us -> 0 us
  between operations: 15.7 us -> 1.33 us
  starting transfers between devices: 10.6 us -> 0 us
  loops' own time: 8.15 us -> 0 us
    select_n x265 -> x0, other arithmetic: 310 us -> none  [the longest x264 310 us: lap(): return jax.tree.map(lambda a, b: jnp.where(reached, a, b), new, before)]
    all_gather x2 -> x0, waiting for transfers between devices: 307 us -> none  [carried_in(): everything = jax.tree.map(lambda part: lax.all_gather(part, axis), shard)]
    all_gather x2 -> x0, blocking collectives: 68.8 us -> none  [carried_in(): everything = jax.tree.map(lambda part: lax.all_gather(part, axis), shard)]
    pallas_call x0 -> x1, Pallas kernels: none -> 51 us  [call(): pl.pallas_call(functools.partial(kernel, NY, NZ), out_shape=jax.ShapeDtyp...]
    dot_general x17 -> x0, matrix products: 16.5 us -> none  [the longest x2 4.32 us: prepare(): joined = jnp.dot(normed, proj_xz, preferred_element_type=jnp.float32)]
    all_to_all x2 -> x0, waiting for transfers between devices: 13.4 us -> none  [the longest x1 13.4 us: local(): lax.all_to_all(send_rows, 'curve', split_axis=0, concat_axis=0, tiled=True)]
    all_to_all x2 -> x0, starting transfers between devices: 10.6 us -> none  [the longest x1 6.41 us: local(): lax.all_to_all(send_slots, 'curve', split_axis=0, concat_axis=0, tiled=True)]
    another operation x2 -> x0, loops' own time: 8.15 us -> none  [carried_in(): return lax.fori_loop(0, peers, lap, start)]
  transfers between devices with their start and end apart: 4 -> 0, of which waited for: 3 -> 0; matrix products, arithmetic and copies ran while one was open for 2% -> 0% of each run, Pallas kernels for 0% -> 0%
where the time goes in v1:
time: 61.3 us; the launch traced here: 60.9 us
  Pallas kernels  51 us (83%)
  local copies, waits for them, and re-layouts  8.53 us (14%)
  between operations  1.33 us (2%)
    pallas_call x1, Pallas kernels, call(): pl.pallas_call(functools.partial(kernel, NY, NZ), out_shape=jax.ShapeDtyp...  51 us
    unnamed x18, local copies, waits for them, and re-layouts  8.53 us

profile of v1, /device:TPU:1, one launch (start us, length us, event | category | flops | bytes accessed | tf_op | source)
XLA Modules:
  0.0 60.9 jit_solution(2936843012065349390)
XLA Ops:
  1.3 0.9 %copy.13.wdt_h = bf16[2,512,16]{2,1,0:T(8,128)(2,1)S(1)} copy(bf16[2,512,16]{1,2,0:T(8,128)(2,1)} %param.19) | data formatting | bytes 65536 | tf_op args[7]
  2.2 0.0 copy-start
  2.2 1.6 %copy-done = bf16[2,1024,512]{2,1,0:T(8,128)(2,1)S(1)} copy-done((bf16[2,1024,512]{2,1,0:T(8,128)(2,1)S(1)}, bf16[2,1024,512]{2,1,0:T(8,128)(2,1)}, u32[]{:S(2)}) %copy-start) | copy-done | bytes 2097176
  3.8 0.0 copy-start.1
  3.8 1.0 %copy-done.1 = bf16[2,512,256]{2,1,0:T(8,128)(2,1)S(1)} copy-done((bf16[2,512,256]{2,1,0:T(8,128)(2,1)S(1)}, bf16[2,512,256]{2,1,0:T(8,128)(2,1)}, u32[]{:S(2)}) %copy-start.1) | copy-done | bytes 524312
  4.9 0.0 copy-start.2
  4.9 0.9 %copy-done.2 = bf16[1,128,512]{2,1,0:T(8,128)(2,1)S(1)} copy-done((bf16[1,128,512]{2,1,0:T(8,128)(2,1)S(1)}, bf16[1,128,512]{2,1,0:T(8,128)(2,1)}, u32[]{:S(2)}) %copy-start.2) | copy-done | bytes 131096
  5.8 0.0 copy-start.3
  5.8 0.7 %copy-done.3 = f32[2,1024]{1,0:T(2,128)S(1)} copy-done((f32[2,1024]{1,0:T(2,128)S(1)}, f32[2,1024]{1,0:T(2,128)}, u32[]{:S(2)}) %copy-start.3) | copy-done | bytes 8216
  6.5 0.0 copy-start.4
  6.5 0.7 %copy-done.4 = f32[2,512]{1,0:T(2,128)S(1)} copy-done((f32[2,512]{1,0:T(2,128)S(1)}, f32[2,512]{1,0:T(2,128)}, u32[]{:S(2)}) %copy-start.4) | copy-done | bytes 4120
  7.2 0.0 copy-start.5
  7.2 0.7 %copy-done.5 = f32[2,16]{1,0:T(2,128)S(1)} copy-done((f32[2,16]{1,0:T(2,128)S(1)}, f32[2,16]{1,0:T(2,128)}, u32[]{:S(2)}) %copy-start.5) | copy-done | bytes 152
  7.8 0.0 copy-start.6
  7.8 0.7 %copy-done.6 = f32[2,16]{1,0:T(2,128)S(1)} copy-done((f32[2,16]{1,0:T(2,128)S(1)}, f32[2,16]{1,0:T(2,128)}, u32[]{:S(2)}) %copy-start.6) | copy-done | bytes 152
  8.5 0.0 copy-start.7
  8.5 0.7 %copy-done.7 = f32[2,16]{1,0:T(2,128)S(1)} copy-done((f32[2,16]{1,0:T(2,128)S(1)}, f32[2,16]{1,0:T(2,128)}, u32[]{:S(2)}) %copy-start.7) | copy-done | bytes 152
  9.2 51.0 %shard_map.118 = bf16[1,128,512]{2,1,0:T(8,128)(2,1)S(1)} custom-call(s32[1,1]{1,0:T(1,128)S(6)} %copy.15.valid_s, s32[1,1,1]{2,1,0:T(1,128)S(6)} %copy.16.dest_s, bf16[1,128,512]{2,1,0:T(8,128)(2,1)S(1)} %copy-done.2, f32[2,512]{1,0:T(2,128)S(1)} %copy-done.4, bf16[2,512,2048]{2,1,0:T(8,128)(2,1)} %wxz_h.1, bf16[2,512,256]{2,1,0:T(8,128)(2,1)S(1)} %copy-done.1, ...), custom_call_target="tpu_custom_call" | custom-call | tf_op jit(solution)/shard_map/pallas_call | solution.py:523
  60.2 0.7 %copy.17 = bf16[1,128,512]{2,1,0:T(8,128)(2,1)} copy(bf16[1,128,512]{2,1,0:T(8,128)(2,1)S(1)} %shard_map.118) | data formatting | bytes 262144
Async XLA Ops:
  2.2 1.6 %copy-start = (bf16[2,1024,512]{2,1,0:T(8,128)(2,1)S(1)}, bf16[2,1024,512]{2,1,0:T(8,128)(2,1)}, u32[]{:S(2)}) copy-start(bf16[2,1024,512]{2,1,0:T(8,128)(2,1)} %wout_h.1) | copy-start | bytes 6291460
  3.8 1.0 %copy-start.1 = (bf16[2,512,256]{2,1,0:T(8,128)(2,1)S(1)}, bf16[2,512,256]{2,1,0:T(8,128)(2,1)}, u32[]{:S(2)}) copy-start(bf16[2,512,256]{2,1,0:T(8,128)(2,1)} %wbc_h.1) | copy-start | bytes 1572868
  4.9 0.9 %copy-start.2 = (bf16[1,128,512]{2,1,0:T(8,128)(2,1)S(1)}, bf16[1,128,512]{2,1,0:T(8,128)(2,1)}, u32[]{:S(2)}) copy-start(bf16[1,128,512]{2,1,0:T(8,128)(2,1)} %x_h.1) | copy-start | bytes 393220
  5.8 0.7 %copy-start.3 = (f32[2,1024]{1,0:T(2,128)S(1)}, f32[2,1024]{1,0:T(2,128)}, u32[]{:S(2)}) copy-start(f32[2,1024]{1,0:T(2,128)} %gg_h.1) | copy-start | bytes 24580
  6.5 0.7 %copy-start.4 = (f32[2,512]{1,0:T(2,128)S(1)}, f32[2,512]{1,0:T(2,128)}, u32[]{:S(2)}) copy-start(f32[2,512]{1,0:T(2,128)} %ng_h.1) | copy-start | bytes 12292
  7.2 0.7 %copy-start.5 = (f32[2,16]{1,0:T(2,128)S(1)}, f32[2,16]{1,0:T(2,128)}, u32[]{:S(2)}) copy-start(f32[2,16]{1,0:T(2,128)} %dtb_h.1) | copy-start | bytes 388
  7.8 0.7 %copy-start.6 = (f32[2,16]{1,0:T(2,128)S(1)}, f32[2,16]{1,0:T(2,128)}, u32[]{:S(2)}) copy-start(f32[2,16]{1,0:T(2,128)} %rate_h.1) | copy-start | bytes 388
  8.5 0.7 %copy-start.7 = (f32[2,16]{1,0:T(2,128)S(1)}, f32[2,16]{1,0:T(2,128)}, u32[]{:S(2)}) copy-start(f32[2,16]{1,0:T(2,128)} %skip_h.1) | copy-start | bytes 388

commit v2 on v1

--- a/solution.py
+++ b/solution.py
@@ -168,7 +168,6 @@
         1.0,
         0.0,
     )
-    rep_b = rep.astype(BF16)
 
     def widen(v):
         hi = v.astype(BF16).astype(F32)
@@ -197,10 +196,11 @@
         return (w * lax.rsqrt(ms + 1e-05) * ng[layer : layer + 1, :]).astype(BF16)
 
     def times_of(nb, live, layer):
-        wrep = jnp.dot(wdt[layer], rep_b, preferred_element_type=F32).astype(BF16)
-        steps = softplus(
-            jnp.dot(nb, wrep, preferred_element_type=F32) + bias8[layer : layer + 1, :]
-        )
+        wrep = jnp.concatenate([wdt[layer]] * 8, axis=0)
+        raw = lax.dot_general(
+            nb, wrep, (((1,), (1,)), ((), ())), preferred_element_type=F32
+        )
+        steps = softplus(raw + bias8[layer : layer + 1, :])
         steps = steps * live
         running = jnp.dot(
             tri, -steps * rate8[layer : layer + 1, :], precision=HI, preferred_element_type=F32
@@ -518,19 +518,19 @@
     RZ = R // NZ
     V = pltpu.VMEM
     DMA = pltpu.SemaphoreType.DMA
-    any_spec = pl.BlockSpec(memory_space=pl.ANY)
+    hbm = pl.BlockSpec(memory_space=pltpu.HBM)
     smem = pl.BlockSpec(memory_space=pltpu.SMEM)
     return pl.pallas_call(
         functools.partial(kernel, NY, NZ),
         out_shape=jax.ShapeDtypeStruct(points.shape, points.dtype),
-        in_specs=[smem, smem] + [any_spec] * 10,
-        out_specs=any_spec,
+        in_specs=[smem, smem] + [hbm] * 10,
+        out_specs=hbm,
         scratch_shapes=[
             V((R, D), BF16),
             V((2, D), F32),
             V((2, 2 * E // CH, D, CH), BF16),
             V((2, D, 2 * R), BF16),
-            V((2, D, H), BF16),
+            V((2, H, D), BF16),
             V((2, H), F32),
             V((2, H), F32),
             V((2, H), F32),
@@ -578,7 +578,7 @@
             DMA(()),
         ],
         compiler_params=pltpu.CompilerParams(
-            collective_id=0, has_side_effects=True, vmem_limit_bytes=48 * 1024 * 1024
+            collective_id=0, has_side_effects=True, vmem_limit_bytes=67043328
         ),
     )(valid_rows, dest_shard, points, *params)
 
@@ -588,8 +588,9 @@
     NZ = min(8, max(1, tiles // 2))
     NY = tiles // NZ
 
-    def local(points, valid_rows, dest_shard, dest_slot, *params):
-        return call(NY, NZ, points, valid_rows, dest_shard, *params)
+    def local(points, valid_rows, dest_shard, dest_slot, ng, wxz, wbc, wdt, *params):
+        wdt = jnp.transpose(wdt, (0, 2, 1))
+        return call(NY, NZ, points, valid_rows, dest_shard, ng, wxz, wbc, wdt, *params)
 
     in_specs = (
         P("tile", "curve", None),

time: 61.3 us -> 54.5 us (0.89)
  local copies, waits for them, and re-layouts: 8.53 us -> 1.57 us
    unnamed x18 -> x1, local copies, waits for them, and re-layouts: 8.53 us -> 1.57 us
where the time goes in v2:
time: 54.5 us; the launch traced here: 54.3 us
  Pallas kernels  51.5 us (94%)
  local copies, waits for them, and re-layouts  1.57 us (3%)
  between operations  1.3 us (2%)
    pallas_call x1, Pallas kernels, call(): pl.pallas_call(functools.partial(kernel, NY, NZ), out_shape=jax.ShapeDtyp...  51.5 us
    unnamed x1, local copies, waits for them, and re-layouts  1.57 us

profile of v2, /device:TPU:1, one launch (start us, length us, event | category | flops | bytes accessed | tf_op | source)
XLA Modules:
  0.0 54.3 jit_solution(4981762579782352425)
XLA Ops:
  1.3 51.5 %shard_map.118 = bf16[1,128,512]{2,1,0:T(8,128)(2,1)} custom-call(s32[1,1]{1,0:T(1,128)S(6)} %copy.14.valid_s, s32[1,1,1]{2,1,0:T(1,128)S(6)} %copy.15.dest_s, bf16[1,128,512]{2,1,0:T(8,128)(2,1)} %x_h.1, f32[2,512]{1,0:T(2,128)} %ng_h.1, bf16[2,512,2048]{2,1,0:T(8,128)(2,1)} %wxz_h.1, bf16[2,512,256]{2,1,0:T(8,128)(2,1)} %wbc_h.1, ...), custom_call_target="tpu_custom_call" | custom-call | tf_op jit(solution)/shard_map/pallas_call | solution.py:523
  52.8 1.6 %copy.16 = bf16[1,128,512]{2,1,0:T(8,128)(2,1)} copy(bf16[1,128,512]{2,1,0:T(8,128)(2,1)} %shard_map.118) | data formatting | bytes 262144

commit v3 on v2

v3 whole, which is shorter than its diff:
```python
import functools

import jax
import jax.numpy as jnp
from jax import lax
from jax.experimental import pallas as pl
from jax.experimental.pallas import tpu as pltpu
from jax.sharding import PartitionSpec as P

F32 = jnp.float32
BF16 = jnp.bfloat16
HI = lax.Precision.HIGHEST
NC = 8
R = 128
D = 512
E = 1024
H = 16
CH = 512


def silu(v):
    return v * jax.nn.sigmoid(v)


def softplus(v):
    return jnp.maximum(v, 0.0) + jnp.log1p(jnp.exp(-jnp.abs(v)))


def mesh_copy(src, dst, send_sem, recv_sem, tile, curve):
    return pltpu.make_async_remote_copy(
        src_ref=src,
        dst_ref=dst,
        send_sem=send_sem,
        recv_sem=recv_sem,
        device_id=(tile, curve),
        device_id_type=pl.DeviceIdType.MESH,
    )


def kernel(
    NY,
    NZ,
    valid_s,
    dest_s,
    x_h,
    ng_h,
    wxz_h,
    wbc_h,
    wdt_h,
    dtb_h,
    rate_h,
    skip_h,
    gg_h,
    wout_h,
    out_h,
    x_v,
    ng,
    wxz,
    wbc,
    wdt,
    dtb,
    rate,
    skip,
    gg,
    wout,
    in_sem,
    exp_m,
    vals,
    gate,
    inner,
    decx,
    scaled,
    sA,
    rA,
    lS,
    lR,
    iS,
    iR,
    sC,
    rC,
    pre,
    lpre,
    tS,
    tR,
    sB1,
    rB1,
    sB3,
    rB3,
    mS,
    mR,
    pS,
    pR,
    a_send,
    a_recv,
    l_send,
    l_recv,
    i_send,
    i_recv,
    c_send,
    c_recv,
    t_send,
    t_recv,
    b1_send,
    b1_recv,
    b3_send,
    b3_recv,
    m_send,
    m_recv,
    ready,
):
    t = lax.axis_index("tile")
    c = lax.axis_index("curve")
    y = t // NZ
    z = lax.rem(t, NZ)
    RZ = R // NZ
    curve_peer = [lax.rem(c + k, NC) for k in range(NC)]
    z_peer = [lax.rem(z + k, NZ) for k in range(NZ)]
    far_first = (4, 5, 3, 2, 6, 7, 1)

    n_in = [0]

    def fetch(src, dst):
        cp = pltpu.make_async_copy(src, dst, in_sem.at[n_in[0]])
        n_in[0] += 1
        cp.start()
        return cp

    def fetch_xz(layer):
        return [
            fetch(wxz_h.at[layer, :, pl.ds(q * CH, CH)], wxz.at[layer, q])
            for q in range(2 * E // CH)
        ]

    x_cp = fetch(x_h.at[0], x_v)
    dt_cp = [fetch(wdt_h.at[0], wdt.at[0])]
    small_cp = [
        fetch(a, b)
        for a, b in ((ng_h, ng), (dtb_h, dtb), (rate_h, rate), (skip_h, skip), (gg_h, gg))
    ]
    bc_cp = [fetch(wbc_h.at[0], wbc.at[0])]
    xz_cp = [fetch_xz(0)]
    out_cp = [fetch(wout_h.at[0], wout.at[0])]

    barrier = pltpu.get_barrier_semaphore()

    def signal(sem, tile, curve):
        pl.semaphore_signal(
            sem, inc=1, device_id=(tile, curve), device_id_type=pl.DeviceIdType.MESH
        )

    for k in range(1, NC):
        signal(barrier, t, curve_peer[k])
    for k in range(1, NZ):
        signal(barrier, y * NZ + z_peer[k], c)
    for a in range(1, NY):

        @pl.when(y + a < NY)
        def _():
            for k in range(NZ):
                signal(barrier, (y + a) * NZ + k, c)

    lane = lax.broadcasted_iota(jnp.int32, (R, R), 1)
    row = lax.broadcasted_iota(jnp.int32, (R, R), 0)
    row_f = row.astype(F32)
    causal = row >= lane
    tri = jnp.where(causal, 1.0, 0.0).astype(F32)
    for j in range(NC):
        exp_m[j] = jnp.where(
            jnp.logical_and(row < 48, (row & 15) == (lane >> 6) + 2 * j), 1.0, 0.0
        ).astype(BF16)
    rep = jnp.where(
        lax.broadcasted_iota(jnp.int32, (H, R), 0)
        == (lax.broadcasted_iota(jnp.int32, (H, R), 1) & 15),
        1.0,
        0.0,
    )

    def parts_of(v):
        hi = v.astype(BF16).astype(F32)
        rest = v - hi
        mid = rest.astype(BF16).astype(F32)
        low = rest - mid
        ln = lax.broadcasted_iota(jnp.int32, v.shape, 1)
        return jnp.where(ln < 16, hi, jnp.where(ln < 32, mid, low)).astype(BF16)

    def widen(parts, j):
        return jnp.dot(parts, exp_m[j], preferred_element_type=F32)

    def copies8(v):
        return jnp.dot(v, rep, precision=HI, preferred_element_type=F32)

    valid_row = jnp.full((1, R), valid_s[0, 0], jnp.int32).astype(F32)
    dest_row = jnp.full((1, R), dest_s[0, 0, 0], jnp.int32).astype(F32)
    iS[0:1, :] = dest_row
    iS[1:2, :] = valid_row

    def norm_of(xb, layer):
        w = xb.astype(F32)
        ms = jnp.mean(w * w, axis=-1, keepdims=True)
        return (w * lax.rsqrt(ms + 1e-05) * ng[layer : layer + 1, :]).astype(BF16)

    def times_of(nb, live, layer):
        wrep = jnp.concatenate([wdt[layer]] * 8, axis=0)
        raw = lax.dot_general(
            nb, wrep, (((1,), (1,)), ((), ())), preferred_element_type=F32
        )
        steps = softplus(raw + bias8[layer : layer + 1, :])
        steps = steps * live
        running = jnp.dot(
            tri, -steps * rate8[layer : layer + 1, :], precision=HI, preferred_element_type=F32
        )
        return steps, running

    def project_values(nb, layer):
        for q in range(E // CH):
            v = silu(jnp.dot(nb, wxz[layer, q], preferred_element_type=F32)).astype(BF16)
            for i in range(CH // R):
                vals[q * (CH // R) + i] = v[:, i * R : (i + 1) * R]

    def project_gate(nb, layer):
        for q in range(E // CH):
            v = silu(jnp.dot(nb, wxz[layer, q + E // CH], preferred_element_type=F32))
            for i in range(CH // R):
                gate[q * (CH // R) + i] = v[:, i * R : (i + 1) * R]

    def keys_of(nb, layer):
        return silu(jnp.dot(nb, wbc[layer, :, 0:R], preferred_element_type=F32))

    def queries_of(nb, layer):
        return silu(jnp.dot(nb, wbc[layer, :, R : 2 * R], preferred_element_type=F32)).astype(BF16)

    sent = []

    def go(copy):
        copy.start()
        sent.append(copy)
        return copy

    def arrive(copies):
        for cp in copies:
            cp.wait_recv()

    def fill_logs(layer, running):
        total = parts_of(jnp.broadcast_to(running[R - 1 : R, :], (8, R)))
        for j in range(NC):
            lS[layer, j] = widen(total, j)[0:1, :]

    def send_logs(layer):
        got = []
        for k in far_first:
            got.append(
                go(
                    mesh_copy(
                        lS.at[layer, curve_peer[k]],
                        lR.at[layer, c],
                        l_send.at[layer, k],
                        l_recv.at[layer, k],
                        t,
                        curve_peer[k],
                    )
                )
            )
        lR[layer, c] = lS[layer, c]
        return got

    def send_states(layer, steps, running, keys):
        wide = parts_of(jnp.exp(running[R - 1 : R, :] - running) * steps)
        keys_t = keys.T.astype(BF16)

        def piece(j):
            scaled = (vals[j].astype(F32) * widen(wide, j)).astype(BF16)
            return jnp.dot(keys_t, scaled, preferred_element_type=F32).astype(BF16)

        got, ready = [], None
        for k in far_first:
            j = curve_peer[k]
            sA[layer, j] = piece(j)
            if ready is not None:
                got.append(go(ready))
            ready = mesh_copy(
                sA.at[layer, j],
                rA.at[layer, c],
                a_send.at[layer, k],
                a_recv.at[layer, k],
                t,
                j,
            )
        rA[layer, c] = piece(c)
        got.append(go(ready))
        return got

    def carried_copy(layer, k):
        return mesh_copy(
            sC.at[layer, curve_peer[k]],
            rC.at[layer, c],
            c_send.at[layer, k],
            c_recv.at[layer, k],
            t,
            curve_peer[k],
        )

    def scores_of(keys, queries):
        scores = lax.dot_general(
            queries, keys.astype(BF16), (((1,), (1,)), ((), ())), preferred_element_type=F32
        )
        return jnp.where(causal, scores, 0.0)

    def inside(layer, steps_t, running, running_t, scores, which):
        half = lane < 64
        wide = parts_of(jnp.exp(running))
        for j in which:
            decx[j] = widen(wide, j)
            vf = vals[j].astype(F32)
            acc = widen(skip_parts, j)[layer : layer + 1, :] * vf
            ws, ves = [], []
            for e in range(2):
                h = 2 * j + e
                gap = running[:, h : h + 1] - running_t[h : h + 1, :]
                w = jnp.exp(jnp.minimum(gap, 0.0)) * steps_t[h : h + 1, :] * scores
                ve = jnp.where(half if e == 0 else jnp.logical_not(half), vf, 0.0)
                ws.append(w.astype(BF16))
                ves.append(ve.astype(BF16))
            inner[j] = acc + jnp.dot(
                jnp.concatenate(ws, axis=1),
                jnp.concatenate(ves, axis=0),
                preferred_element_type=F32,
            )

    def finish(layer, xb, live_col, queries):
        squares = jnp.zeros((R, R), F32)
        for j in range(NC):
            from_state = jnp.dot(queries, rC[layer, j], preferred_element_type=F32)
            g = (inner[j] + decx[j] * from_state) * gate[j]
            squares = squares + g * g
            cols = slice(j * R, (j + 1) * R)
            scaled[:, cols] = (g * gg[layer : layer + 1, cols]).astype(BF16)
        scale = lax.rsqrt(jnp.sum(squares, axis=-1, keepdims=True) * (1.0 / E) + 1e-05)
        update = jnp.dot(scaled[...], wout[layer], preferred_element_type=F32)
        return (xb.astype(F32) + (live_col * scale) * update).astype(BF16)

    live = jnp.where(row_f < valid_row, 1.0, 0.0)
    x_cp.wait()
    for cp in small_cp:
        cp.wait()
    for cp in (dt_cp[0], bc_cp[0], xz_cp[0][0], xz_cp[0][1]):
        cp.wait()
    bias8, rate8 = copies8(dtb[...]), copies8(rate[...])
    skip_parts = parts_of(jnp.concatenate([copies8(skip[...])] * 4, axis=0))
    xb = x_v[...]
    nb = norm_of(xb, 0)
    steps, running = times_of(nb, live, 0)
    keys = keys_of(nb, 0)
    project_values(nb, 0)
    fill_logs(0, running)
    pl.semaphore_wait(barrier, (NC - 1) + (NZ - 1) + NZ * y)
    got_l = send_logs(0)
    got = send_states(0, steps, running, keys)
    got_i = []
    for k in far_first:
        got_i.append(
            go(mesh_copy(iS, iR.at[c], i_send.at[k], i_recv.at[k], t, curve_peer[k]))
        )
    iR[c] = iS[...]
    for a in range(1, NY):

        @pl.when(y >= a)
        def _():
            for k in range(NZ):
                signal(ready, (y - a) * NZ + k, c)

    dt_cp.append(fetch(wdt_h.at[1], wdt.at[1]))
    bc_cp.append(fetch(wbc_h.at[1], wbc.at[1]))
    xz_cp.append(fetch_xz(1))
    out_cp.append(fetch(wout_h.at[1], wout.at[1]))
    xz_cp[0][2].wait()
    xz_cp[0][3].wait()
    project_gate(nb, 0)
    queries = queries_of(nb, 0)
    scores = scores_of(keys, queries)
    running_t, steps_t = running.T, steps.T
    arrive(got_l)
    arrive(got)
    state = jnp.zeros((R, R), F32)
    for p in range(NC):
        sC[0, p] = state.astype(BF16)
        if p < NC - 1:
            state = jnp.exp(lR[0, p]) * state + rA[0, p].astype(F32)
    got = [go(carried_copy(0, k)) for k in far_first]
    rC[0, c] = sC[0, c]
    inside(0, steps_t, running, running_t, scores, range(NC))
    out_cp[0].wait()
    dt_cp[1].wait()
    bc_cp[1].wait()
    for cp in xz_cp[1]:
        cp.wait()
    out_cp[1].wait()
    arrive(got_i)
    arrive(got)
    first = finish(0, xb, live[:, 0:1], queries)
    mS[...] = first

    nb = norm_of(first, 1)
    steps, running = times_of(nb, live, 1)
    keys = keys_of(nb, 1)
    project_values(nb, 1)
    fill_logs(1, running)
    got_l = send_logs(1)
    got_a = send_states(1, steps, running, keys)

    got_m = []
    for k in (2, 1, 3):
        got_m.append(
            go(mesh_copy(mS, mR.at[k], m_send.at[k], m_recv.at[k], t, curve_peer[2 * k]))
        )

    def row_sends(start_copy):
        own = [start_copy(0, k) for k in range(1, NZ)]
        for cp in own:
            cp.start()
        later = []
        for a in range(1, NY):
            cps = [start_copy(a, k) for k in range(NZ)]

            @pl.when(y + a < NY)
            def _():
                for cp in cps:
                    cp.start()

            later.append(cps)
        return own, later

    def row_arrive(pair):
        own, later = pair
        arrive(own)
        for a in range(1, NY):

            @pl.when(y >= a)
            def _():
                arrive(later[a - 1])

    def row_sent(pair):
        own, later = pair
        for cp in own:
            cp.wait_send()
        for a in range(1, NY):

            @pl.when(y + a < NY)
            def _():
                for cp in later[a - 1]:
                    cp.wait_send()

    arrive(got_l)
    logs = [lR[1, s] for s in range(NC)]
    place = [iR[s, 0:1, :] for s in range(NC)]
    tile_log = logs[0]
    for s in range(1, NC):
        tile_log = tile_log + logs[s]
    tS[...] = tile_log
    weights = []
    for s in range(NC):
        after = jnp.zeros((1, R), F32)
        for o in range(NC):
            if o != s:
                after = after + jnp.where(place[o] > place[s], logs[o], 0.0)
        weights.append(jnp.exp(after))
    tR[y, z] = tile_log

    @pl.when(y < NY - 1)
    def _():
        pl.semaphore_wait(ready, NZ * (NY - 1 - y))

    logs_sent = row_sends(
        lambda a, k: mesh_copy(
            tS,
            tR.at[y, z],
            t_send.at[a, k],
            t_recv.at[a, k],
            (y + a) * NZ + z_peer[k],
            c,
        )
    )
    arrive(got_a)
    total = weights[0] * rA[1, 0].astype(F32)
    for s in range(1, NC):
        total = total + weights[s] * rA[1, s].astype(F32)
    for k in range(NZ):
        sB1[k] = total[k * RZ : (k + 1) * RZ, :].astype(BF16)
    rB1[y, z] = sB1[z]
    states_sent = row_sends(
        lambda a, k: mesh_copy(
            sB1.at[z_peer[k]],
            rB1.at[y, z],
            b1_send.at[a, k],
            b1_recv.at[a, k],
            (y + a) * NZ + z_peer[k],
            c,
        )
    )

    def lap(p, carry):
        state, log_sum = carry
        pre[p] = state
        lpre[p] = log_sum
        pf = p.astype(F32)
        here = [jnp.where(place[s] == pf, 1.0, 0.0) for s in range(NC)]
        log_p = here[0] * logs[0]
        new = here[0] * rA[1, 0].astype(F32)
        for s in range(1, NC):
            log_p = log_p + here[s] * logs[s]
            new = new + here[s] * rA[1, s].astype(F32)
        return jnp.exp(log_p) * state + new, log_sum + log_p

    lax.fori_loop(0, NC, lap, (jnp.zeros((R, R), F32), jnp.zeros((1, R), F32)))

    row_arrive(logs_sent)
    row_arrive(states_sent)
    state = jnp.zeros((RZ, R), F32)
    for a in range(NY - 1):
        new = state
        for k in range(NZ):
            new = jnp.exp(tR[a, k]) * new + rB1[a, k].astype(F32)
        state = jnp.where(a < y, new, state)
    for k in range(NZ):
        sB3[k] = state.astype(BF16)
        if k < NZ - 1:
            state = jnp.exp(tR[y, k]) * state + rB1[y, k].astype(F32)
    rB3[z] = sB3[z]
    got = []
    for k in (4, 3, 5, 2, 6, 1, 7) if NZ == 8 else range(1, NZ):
        got.append(
            go(
                mesh_copy(
                    sB3.at[z_peer[k]],
                    rB3.at[z],
                    b3_send.at[k],
                    b3_recv.at[k],
                    y * NZ + z_peer[k],
                    c,
                )
            )
        )
    arrive(got_m)
    partner = c + 1 - 2 * lax.rem(c, 2)
    c_f, partner_f = c.astype(F32), partner.astype(F32)
    mine = jnp.zeros((R, D), F32)
    theirs = jnp.zeros((R, D), F32)
    for k in range(4):
        goes = iR[lax.rem(c + NC - 2 * k, NC), 0:1, :]
        blk = (mS[...] if k == 0 else mR[k]).astype(F32)
        m_mine = jnp.concatenate([jnp.where(goes == c_f, 1.0, 0.0)] * 4, axis=1)
        m_theirs = jnp.concatenate([jnp.where(goes == partner_f, 1.0, 0.0)] * 4, axis=1)
        mine = mine + m_mine * blk
        theirs = theirs + m_theirs * blk
    pS[...] = theirs.astype(BF16)
    x_v[...] = mine.astype(BF16)
    valid_row = jnp.zeros((1, R), F32)
    for s in range(NC):
        valid_row = valid_row + jnp.where(place[s] == c_f, 1.0, 0.0) * iR[s, 1:2, :]
    live = jnp.where(row_f < valid_row, 1.0, 0.0)
    swap = go(mesh_copy(pS, pR, m_send.at[0], m_recv.at[0], t, partner))

    swap.wait_recv()
    xb = (x_v[...].astype(F32) + pR[...].astype(F32)).astype(BF16)
    nb = norm_of(xb, 1)
    steps, running = times_of(nb, live, 1)
    keys = keys_of(nb, 1)
    queries = queries_of(nb, 1)
    project_values(nb, 1)

    project_gate(nb, 1)
    scores = scores_of(keys, queries)
    running_t, steps_t = running.T, steps.T
    arrive(got)
    entry = jnp.concatenate([rB3[k].astype(F32) for k in range(NZ)], axis=0)
    got, ready = [], None
    for k in far_first:
        p = curve_peer[k]
        sC[1, p] = (jnp.exp(lpre[p]) * entry + pre[p]).astype(BF16)
        if ready is not None:
            got.append(go(ready))
        ready = carried_copy(1, k)
    rC[1, c] = (jnp.exp(lpre[c]) * entry + pre[c]).astype(BF16)
    got.append(go(ready))
    inside(1, steps_t, running, running_t, scores, range(NC))
    last = {id(cp) for cp in got}
    for cp in sent:
        if id(cp) not in last:
            cp.wait_send()
    row_sent(logs_sent)
    row_sent(states_sent)
    arrive(got)
    out_h[0] = finish(1, xb, live[:, 0:1], queries)
    for cp in got:
        cp.wait_send()


def call(NY, NZ, points, valid_rows, dest_shard, *params):
    RZ = R // NZ
    V = pltpu.VMEM
    DMA = pltpu.SemaphoreType.DMA
    hbm = pl.BlockSpec(memory_space=pltpu.HBM)
    smem = pl.BlockSpec(memory_space=pltpu.SMEM)
    return pl.pallas_call(
        functools.partial(kernel, NY, NZ),
        out_shape=jax.ShapeDtypeStruct(points.shape, points.dtype),
        in_specs=[smem, smem] + [hbm] * 10,
        out_specs=pl.BlockSpec(memory_space=pltpu.VMEM),
        scratch_shapes=[
            V((R, D), BF16),
            V((2, D), F32),
            V((2, 2 * E // CH, D, CH), BF16),
            V((2, D, 2 * R), BF16),
            V((2, H, D), BF16),
            V((2, H), F32),
            V((2, H), F32),
            V((2, H), F32),
            V((2, E), F32),
            V((2, E, D), BF16),
            DMA((20,)),
            V((NC, R, R), BF16),
            V((NC, R, R), BF16),
            V((NC, R, R), F32),
            V((NC, R, R), F32),
            V((NC, R, R), F32),
            V((R, E), BF16),
            V((2, NC, R, R), BF16),
            V((2, NC, R, R), BF16),
            V((2, NC, 1, R), F32),
            V((2, NC, 1, R), F32),
            V((2, R), F32),
            V((NC, 2, R), F32),
            V((2, NC, R, R), BF16),
            V((2, NC, R, R), BF16),
            V((NC, R, R), F32),
            V((NC, 1, R), F32),
            V((1, R), F32),
            V((NY, NZ, 1, R), F32),
            V((NZ, RZ, R), BF16),
            V((NY, NZ, RZ, R), BF16),
            V((NZ, RZ, R), BF16),
            V((NZ, RZ, R), BF16),
            V((R, D), BF16),
            V((4, R, D), BF16),
            V((R, D), BF16),
            V((R, D), BF16),
            DMA((2, NC)),
            DMA((2, NC)),
            DMA((2, NC)),
            DMA((2, NC)),
            DMA((NC,)),
            DMA((NC,)),
            DMA((2, NC)),
            DMA((2, NC)),
            DMA((NY, NZ)),
            DMA((NY, NZ)),
            DMA((NY, NZ)),
            DMA((NY, NZ)),
            DMA((NZ,)),
            DMA((NZ,)),
            DMA((4,)),
            DMA((4,)),
            pltpu.SemaphoreType.REGULAR,
        ],
        compiler_params=pltpu.CompilerParams(
            collective_id=0, has_side_effects=True, vmem_limit_bytes=40 * 1024 * 1024
        ),
    )(valid_rows, dest_shard, *[pltpu.with_memory_space_constraint(v, pltpu.HBM) for v in (points, *params)])


def solution(mesh):
    tiles = mesh.shape["tile"]
    NZ = min(8, max(1, tiles // 2))
    NY = tiles // NZ

    def local(points, valid_rows, dest_shard, dest_slot, ng, wxz, wbc, wdt, *params):
        wdt = jnp.transpose(wdt, (0, 2, 1))
        return call(NY, NZ, points, valid_rows, dest_shard, ng, wxz, wbc, wdt, *params)

    in_specs = (
        P("tile", "curve", None),
        P("tile", "curve"),
        P("tile", "curve", None),
        P("tile", "curve", None),
    ) + (P(),) * 9
    return jax.shard_map(
        local, mesh=mesh, in_specs=in_specs, out_specs=P("tile", "curve", None), check_vma=False
    )
```

time: 54.5 us -> 48 us (0.88)
  Pallas kernels: 51.5 us -> 45.5 us
  local copies, waits for them, and re-layouts: 1.57 us -> 0.66 us
    pallas_call x1, Pallas kernels: 51.5 us -> 45.5 us  [call(): pl.pallas_call(functools.partial(kernel, NY, NZ), out_shape=jax.ShapeDtyp...]
    unnamed x1, local copies, waits for them, and re-layouts: 1.57 us -> 0.66 us
where the time goes in v3:
time: 48 us; the launch traced here: 47.4 us
  Pallas kernels  45.5 us (95%)
  between operations  1.3 us (3%)
  local copies, waits for them, and re-layouts  0.66 us (1%)
    pallas_call x1, Pallas kernels, call(): pl.pallas_call(functools.partial(kernel, NY, NZ), out_shape=jax.ShapeDtyp...  45.5 us

profile of v3, /device:TPU:1, one launch (start us, length us, event | category | flops | bytes accessed | tf_op | source)
XLA Modules:
  0.0 47.4 jit_solution(5618186887467216829)
XLA Ops:
  1.3 45.5 %shard_map.118 = bf16[1,128,512]{2,1,0:T(8,128)(2,1)S(1)} custom-call(s32[1,1]{1,0:T(1,128)S(6)} %copy.14.valid_s, s32[1,1,1]{2,1,0:T(1,128)S(6)} %copy.15.dest_s, bf16[1,128,512]{2,1,0:T(8,128)(2,1)} %x_h.1, f32[2,512]{1,0:T(2,128)} %ng_h.1, bf16[2,512,2048]{2,1,0:T(8,128)(2,1)} %wxz_h.1, bf16[2,512,256]{2,1,0:T(8,128)(2,1)} %wbc_h.1, ...), custom_call_target="tpu_custom_call" | custom-call | tf_op jit(solution)/shard_map/pallas_call | solution.py:603
  46.8 0.7 %copy.16 = bf16[1,128,512]{2,1,0:T(8,128)(2,1)} copy(bf16[1,128,512]{2,1,0:T(8,128)(2,1)S(1)} %shard_map.118) | data formatting | bytes 262144

commit v4 on v3

--- a/solution.py
+++ b/solution.py
@@ -16,6 +16,8 @@
 E = 1024
 H = 16
 CH = 512
+W = 256
+NX = E // W
 
 
 def silu(v):
@@ -40,8 +42,8 @@
 def kernel(
     NY,
     NZ,
-    valid_s,
-    dest_s,
+    valid_v,
+    dest_v,
     x_h,
     ng_h,
     wxz_h,
@@ -69,7 +71,8 @@
     gate,
     inner,
     decx,
-    scaled,
+    acc,
+    ggx,
     sA,
     rA,
     lS,
@@ -115,7 +118,27 @@
     RZ = R // NZ
     curve_peer = [lax.rem(c + k, NC) for k in range(NC)]
     z_peer = [lax.rem(z + k, NZ) for k in range(NZ)]
+    x = c // 2
+    partner = c + 1 - 2 * lax.rem(c, 2)
     far_first = (4, 5, 3, 2, 6, 7, 1)
+
+    barrier = pltpu.get_barrier_semaphore()
+
+    def signal(sem, tile, curve):
+        pl.semaphore_signal(
+            sem, inc=1, device_id=(tile, curve), device_id_type=pl.DeviceIdType.MESH
+        )
+
+    def each_tile(first, last, sem):
+        def one(i, _):
+            signal(sem, i, c)
+            return 0
+
+        lax.fori_loop(first, last, one, 0)
+
+    for k in range(1, NC):
+        signal(barrier, t, curve_peer[k])
+    each_tile(t + 1, NY * NZ, barrier)
 
     n_in = [0]
 
@@ -131,41 +154,22 @@
             for q in range(2 * E // CH)
         ]
 
+    small_cp = [fetch(a, b) for a, b in ((dtb_h, dtb), (rate_h, rate), (skip_h, skip))]
     x_cp = fetch(x_h.at[0], x_v)
+    small_cp += [fetch(ng_h, ng)]
     dt_cp = [fetch(wdt_h.at[0], wdt.at[0])]
-    small_cp = [
-        fetch(a, b)
-        for a, b in ((ng_h, ng), (dtb_h, dtb), (rate_h, rate), (skip_h, skip), (gg_h, gg))
-    ]
+    xz_cp = [fetch_xz(0)]
     bc_cp = [fetch(wbc_h.at[0], wbc.at[0])]
-    xz_cp = [fetch_xz(0)]
+    small_cp += [fetch(gg_h, gg)]
     out_cp = [fetch(wout_h.at[0], wout.at[0])]
-
-    barrier = pltpu.get_barrier_semaphore()
-
-    def signal(sem, tile, curve):
-        pl.semaphore_signal(
-            sem, inc=1, device_id=(tile, curve), device_id_type=pl.DeviceIdType.MESH
-        )
-
-    for k in range(1, NC):
-        signal(barrier, t, curve_peer[k])
-    for k in range(1, NZ):
-        signal(barrier, y * NZ + z_peer[k], c)
-    for a in range(1, NY):
-
-        @pl.when(y + a < NY)
-        def _():
-            for k in range(NZ):
-                signal(barrier, (y + a) * NZ + k, c)
 
     lane = lax.broadcasted_iota(jnp.int32, (R, R), 1)
     row = lax.broadcasted_iota(jnp.int32, (R, R), 0)
     row_f = row.astype(F32)
     causal = row >= lane
-    tri = jnp.where(causal, 1.0, 0.0).astype(F32)
+    tri = jnp.concatenate([jnp.where(causal, 1.0, 0.0).astype(BF16)] * 3, axis=1)
     for j in range(NC):
-        exp_m[j] = jnp.where(
+        exp_m[j // 2, :, (j % 2) * R : (j % 2 + 1) * R] = jnp.where(
             jnp.logical_and(row < 48, (row & 15) == (lane >> 6) + 2 * j), 1.0, 0.0
         ).astype(BF16)
     rep = jnp.where(
@@ -183,16 +187,12 @@
         ln = lax.broadcasted_iota(jnp.int32, v.shape, 1)
         return jnp.where(ln < 16, hi, jnp.where(ln < 32, mid, low)).astype(BF16)
 
-    def widen(parts, j):
-        return jnp.dot(parts, exp_m[j], preferred_element_type=F32)
+    def widen(parts, q):
+        return jnp.dot(parts, exp_m[q], preferred_element_type=F32)
 
     def copies8(v):
         return jnp.dot(v, rep, precision=HI, preferred_element_type=F32)
 
-    valid_row = jnp.full((1, R), valid_s[0, 0], jnp.int32).astype(F32)
-    dest_row = jnp.full((1, R), dest_s[0, 0, 0], jnp.int32).astype(F32)
-    iS[0:1, :] = dest_row
-    iS[1:2, :] = valid_row
 
     def norm_of(xb, layer):
         w = xb.astype(F32)
@@ -206,22 +206,27 @@
         )
         steps = softplus(raw + bias8[layer : layer + 1, :])
         steps = steps * live
+        fall = -steps * rate8[layer : layer + 1, :]
+        hi = fall.astype(BF16)
+        rest = fall - hi.astype(F32)
+        mid = rest.astype(BF16)
+        low = (rest - mid.astype(F32)).astype(BF16)
         running = jnp.dot(
-            tri, -steps * rate8[layer : layer + 1, :], precision=HI, preferred_element_type=F32
+            tri, jnp.concatenate([hi, mid, low], axis=0), preferred_element_type=F32
         )
         return steps, running
 
     def project_values(nb, layer):
         for q in range(E // CH):
             v = silu(jnp.dot(nb, wxz[layer, q], preferred_element_type=F32)).astype(BF16)
-            for i in range(CH // R):
-                vals[q * (CH // R) + i] = v[:, i * R : (i + 1) * R]
+            for i in range(CH // W):
+                vals[q * (CH // W) + i] = v[:, i * W : (i + 1) * W]
 
     def project_gate(nb, layer):
         for q in range(E // CH):
             v = silu(jnp.dot(nb, wxz[layer, q + E // CH], preferred_element_type=F32))
-            for i in range(CH // R):
-                gate[q * (CH // R) + i] = v[:, i * R : (i + 1) * R]
+            for i in range(CH // W):
+                gate[q * (CH // W) + i] = v[:, i * W : (i + 1) * W]
 
     def keys_of(nb, layer):
         return silu(jnp.dot(nb, wbc[layer, :, 0:R], preferred_element_type=F32))
@@ -242,8 +247,10 @@
 
     def fill_logs(layer, running):
         total = parts_of(jnp.broadcast_to(running[R - 1 : R, :], (8, R)))
-        for j in range(NC):
-            lS[layer, j] = widen(total, j)[0:1, :]
+        for q in range(NX):
+            wide = widen(total, q)
+            lS[layer, 2 * q] = wide[0:1, :R]
+            lS[layer, 2 * q + 1] = wide[0:1, R:]
 
     def send_logs(layer):
         got = []
@@ -263,31 +270,41 @@
         lR[layer, c] = lS[layer, c]
         return got
 
-    def send_states(layer, steps, running, keys):
+    def make_states(layer, steps, running, keys):
         wide = parts_of(jnp.exp(running[R - 1 : R, :] - running) * steps)
         keys_t = keys.T.astype(BF16)
 
-        def piece(j):
-            scaled = (vals[j].astype(F32) * widen(wide, j)).astype(BF16)
-            return jnp.dot(keys_t, scaled, preferred_element_type=F32).astype(BF16)
-
-        got, ready = [], None
-        for k in far_first:
-            j = curve_peer[k]
-            sA[layer, j] = piece(j)
-            if ready is not None:
-                got.append(go(ready))
-            ready = mesh_copy(
-                sA.at[layer, j],
-                rA.at[layer, c],
-                a_send.at[layer, k],
-                a_recv.at[layer, k],
-                t,
-                j,
+        for q in range(NX):
+            scaled = (vals[q].astype(F32) * widen(wide, q)).astype(BF16)
+            both = jnp.dot(keys_t, scaled, preferred_element_type=F32).astype(BF16)
+            sA[layer, 2 * q] = both[:, :R]
+            sA[layer, 2 * q + 1] = both[:, R:]
+
+    def send_states(layer):
+        got_l, got = send_logs(layer), []
+
+        def send(j):
+            k = lax.rem(j - c + NC, NC)
+            got.append(
+                go(
+                    mesh_copy(
+                        sA.at[layer, j],
+                        rA.at[layer, c],
+                        a_send.at[layer, k],
+                        a_recv.at[layer, k],
+                        t,
+                        j,
+                    )
+                )
             )
-        rA[layer, c] = piece(c)
-        got.append(go(ready))
-        return got
+
+        chip = [lax.rem(x + d, NX) for d in range(NX)]
+        for d in (2, 1, 3):
+            send(2 * chip[d])
+            send(2 * chip[d] + 1)
+        send(partner)
+        rA[layer, c] = sA[layer, c]
+        return got_l, got
 
     def carried_copy(layer, k):
         return mesh_copy(
@@ -308,66 +325,87 @@
     def inside(layer, steps_t, running, running_t, scores, which):
         half = lane < 64
         wide = parts_of(jnp.exp(running))
-        for j in which:
-            decx[j] = widen(wide, j)
-            vf = vals[j].astype(F32)
-            acc = widen(skip_parts, j)[layer : layer + 1, :] * vf
-            ws, ves = [], []
-            for e in range(2):
-                h = 2 * j + e
-                gap = running[:, h : h + 1] - running_t[h : h + 1, :]
-                w = jnp.exp(jnp.minimum(gap, 0.0)) * steps_t[h : h + 1, :] * scores
-                ve = jnp.where(half if e == 0 else jnp.logical_not(half), vf, 0.0)
-                ws.append(w.astype(BF16))
-                ves.append(ve.astype(BF16))
-            inner[j] = acc + jnp.dot(
-                jnp.concatenate(ws, axis=1),
-                jnp.concatenate(ves, axis=0),
-                preferred_element_type=F32,
-            )
+        for q in which:
+            decx[q] = widen(wide, q)
+            skips = widen(skip_parts, q)[layer : layer + 1, :]
+            for j in (2 * q, 2 * q + 1):
+                cols = slice((j % 2) * R, (j % 2 + 1) * R)
+                vf = vals[q, :, cols].astype(F32)
+                ws, ves = [], []
+                for e in range(2):
+                    h = 2 * j + e
+                    gap = running[:, h : h + 1] - running_t[h : h + 1, :]
+                    w = jnp.exp(jnp.minimum(gap, 0.0)) * steps_t[h : h + 1, :] * scores
+                    ve = jnp.where(half if e == 0 else jnp.logical_not(half), vf, 0.0)
+                    ws.append(w.astype(BF16))
+                    ves.append(ve.astype(BF16))
+                inner[q, :, cols] = skips[:, cols] * vf + jnp.dot(
+                    jnp.concatenate(ws, axis=1),
+                    jnp.concatenate(ves, axis=0),
+                    preferred_element_type=F32,
+                )
 
     def finish(layer, xb, live_col, queries):
-        squares = jnp.zeros((R, R), F32)
-        for j in range(NC):
-            from_state = jnp.dot(queries, rC[layer, j], preferred_element_type=F32)
-            g = (inner[j] + decx[j] * from_state) * gate[j]
+        squares = jnp.zeros((R, W), F32)
+        for d in (0, 1, 3, 2):
+            xs = lax.rem(x + 4 - d, 4)
+            both = (2 * xs, 2 * xs + 1)
+            for src in (partner,) if d == 0 else both:
+                mesh_copy(
+                    sC.at[layer, src],
+                    rC.at[layer, src],
+                    c_send.at[layer, 0],
+                    c_recv.at[layer, lax.rem(c - src + NC, NC)],
+                    t,
+                    src,
+                ).wait_recv()
+            states = jnp.concatenate([rC[layer, both[0]], rC[layer, both[1]]], axis=1)
+            from_state = jnp.dot(queries, states, preferred_element_type=F32)
+            g = (inner[xs] + decx[xs] * from_state) * gate[xs]
             squares = squares + g * g
-            cols = slice(j * R, (j + 1) * R)
-            scaled[:, cols] = (g * gg[layer : layer + 1, cols]).astype(BF16)
+            block = (g * ggx[layer, xs]).astype(BF16)
+            rows = pl.ds(pl.multiple_of(xs * (2 * R), 2 * R), 2 * R)
+            new = jnp.dot(block, wout[layer, rows, :], preferred_element_type=F32)
+            if d == 0:
+                acc[...] = new
+            elif d != 2:
+                acc[...] += new
         scale = lax.rsqrt(jnp.sum(squares, axis=-1, keepdims=True) * (1.0 / E) + 1e-05)
-        update = jnp.dot(scaled[...], wout[layer], preferred_element_type=F32)
+        update = acc[...] + new
         return (xb.astype(F32) + (live_col * scale) * update).astype(BF16)
 
+    for cp in small_cp[:3]:
+        cp.wait()
+    valid_row = jnp.broadcast_to(valid_v[...], (1, R)).astype(F32)
+    iS[0:1, :] = jnp.broadcast_to(dest_v[...], (1, R)).astype(F32)
+    iS[1:2, :] = valid_row
     live = jnp.where(row_f < valid_row, 1.0, 0.0)
+    bias8, rate8 = copies8(dtb[...]), copies8(rate[...])
+    skip_parts = parts_of(jnp.concatenate([copies8(skip[...])] * 4, axis=0))
     x_cp.wait()
-    for cp in small_cp:
-        cp.wait()
+    small_cp[3].wait()
+    xb = x_v[...]
+    nb = norm_of(xb, 0)
     for cp in (dt_cp[0], bc_cp[0], xz_cp[0][0], xz_cp[0][1]):
         cp.wait()
-    bias8, rate8 = copies8(dtb[...]), copies8(rate[...])
-    skip_parts = parts_of(jnp.concatenate([copies8(skip[...])] * 4, axis=0))
-    xb = x_v[...]
-    nb = norm_of(xb, 0)
     steps, running = times_of(nb, live, 0)
     keys = keys_of(nb, 0)
     project_values(nb, 0)
     fill_logs(0, running)
-    pl.semaphore_wait(barrier, (NC - 1) + (NZ - 1) + NZ * y)
-    got_l = send_logs(0)
-    got = send_states(0, steps, running, keys)
+    make_states(0, steps, running, keys)
+    pl.semaphore_wait(barrier, (NC - 1) + t)
+    got_l, got = send_states(0)
     got_i = []
     for k in far_first:
         got_i.append(
             go(mesh_copy(iS, iR.at[c], i_send.at[k], i_recv.at[k], t, curve_peer[k]))
         )
     iR[c] = iS[...]
-    for a in range(1, NY):
-
-        @pl.when(y >= a)
-        def _():
-            for k in range(NZ):
-                signal(ready, (y - a) * NZ + k, c)
-
+    each_tile(0, t, ready)
+    small_cp[4].wait()
+    for layer in range(2):
+        for q in range(NX):
+            ggx[layer, q] = gg[layer : layer + 1, q * W : (q + 1) * W]
     dt_cp.append(fetch(wdt_h.at[1], wdt.at[1]))
     bc_cp.append(fetch(wbc_h.at[1], wbc.at[1]))
     xz_cp.append(fetch_xz(1))
@@ -387,7 +425,7 @@
             state = jnp.exp(lR[0, p]) * state + rA[0, p].astype(F32)
     got = [go(carried_copy(0, k)) for k in far_first]
     rC[0, c] = sC[0, c]
-    inside(0, steps_t, running, running_t, scores, range(NC))
+    inside(0, steps_t, running, running_t, scores, range(NX))
     out_cp[0].wait()
     dt_cp[1].wait()
     bc_cp[1].wait()
@@ -395,7 +433,6 @@
         cp.wait()
     out_cp[1].wait()
     arrive(got_i)
-    arrive(got)
     first = finish(0, xb, live[:, 0:1], queries)
     mS[...] = first
 
@@ -404,8 +441,8 @@
     keys = keys_of(nb, 1)
     project_values(nb, 1)
     fill_logs(1, running)
-    got_l = send_logs(1)
-    got_a = send_states(1, steps, running, keys)
+    make_states(1, steps, running, keys)
+    got_l, got_a = send_states(1)
 
     got_m = []
     for k in (2, 1, 3):
@@ -413,20 +450,21 @@
             go(mesh_copy(mS, mR.at[k], m_send.at[k], m_recv.at[k], t, curve_peer[2 * k]))
         )
 
+    far_z = (4, 3, 5, 2, 6, 1, 7, 0) if NZ == 8 else tuple(range(NZ))
+
     def row_sends(start_copy):
-        own = [start_copy(0, k) for k in range(1, NZ)]
-        for cp in own:
-            cp.start()
-        later = []
-        for a in range(1, NY):
-            cps = [start_copy(a, k) for k in range(NZ)]
+        own = [start_copy(0, k) for k in far_z if k > 0]
+        later = [[start_copy(a, k) for k in far_z] for a in range(1, NY)]
+        for a in (2, 1, 3) if NY == 4 else range(1, NY):
+            cps = later[a - 1]
 
             @pl.when(y + a < NY)
             def _():
                 for cp in cps:
                     cp.start()
 
-            later.append(cps)
+        for cp in own:
+            cp.start()
         return own, later
 
     def row_arrive(pair):
@@ -465,9 +503,9 @@
         weights.append(jnp.exp(after))
     tR[y, z] = tile_log
 
-    @pl.when(y < NY - 1)
+    @pl.when(t < NY * NZ - 1)
     def _():
-        pl.semaphore_wait(ready, NZ * (NY - 1 - y))
+        pl.semaphore_wait(ready, NY * NZ - 1 - t)
 
     logs_sent = row_sends(
         lambda a, k: mesh_copy(
@@ -526,7 +564,7 @@
             state = jnp.exp(tR[y, k]) * state + rB1[y, k].astype(F32)
     rB3[z] = sB3[z]
     got = []
-    for k in (4, 3, 5, 2, 6, 1, 7) if NZ == 8 else range(1, NZ):
+    for k in [k for k in far_z if k > 0]:
         got.append(
             go(
                 mesh_copy(
@@ -540,7 +578,6 @@
             )
         )
     arrive(got_m)
-    partner = c + 1 - 2 * lax.rem(c, 2)
     c_f, partner_f = c.astype(F32), partner.astype(F32)
     mine = jnp.zeros((R, D), F32)
     theirs = jnp.zeros((R, D), F32)
@@ -581,14 +618,13 @@
         ready = carried_copy(1, k)
     rC[1, c] = (jnp.exp(lpre[c]) * entry + pre[c]).astype(BF16)
     got.append(go(ready))
-    inside(1, steps_t, running, running_t, scores, range(NC))
+    inside(1, steps_t, running, running_t, scores, range(NX))
     last = {id(cp) for cp in got}
     for cp in sent:
         if id(cp) not in last:
             cp.wait_send()
     row_sent(logs_sent)
     row_sent(states_sent)
-    arrive(got)
     out_h[0] = finish(1, xb, live[:, 0:1], queries)
     for cp in got:
         cp.wait_send()
@@ -596,14 +632,15 @@
 
 def call(NY, NZ, points, valid_rows, dest_shard, *params):
     RZ = R // NZ
+    operands = (points, *params)
     V = pltpu.VMEM
     DMA = pltpu.SemaphoreType.DMA
     hbm = pl.BlockSpec(memory_space=pltpu.HBM)
-    smem = pl.BlockSpec(memory_space=pltpu.SMEM)
+    vmem = pl.BlockSpec(memory_space=pltpu.VMEM)
     return pl.pallas_call(
         functools.partial(kernel, NY, NZ),
         out_shape=jax.ShapeDtypeStruct(points.shape, points.dtype),
-        in_specs=[smem, smem] + [hbm] * 10,
+        in_specs=[vmem, vmem] + [hbm] * 10,
         out_specs=pl.BlockSpec(memory_space=pltpu.VMEM),
         scratch_shapes=[
             V((R, D), BF16),
@@ -617,12 +654,13 @@
             V((2, E), F32),
             V((2, E, D), BF16),
             DMA((20,)),
-            V((NC, R, R), BF16),
-            V((NC, R, R), BF16),
-            V((NC, R, R), F32),
-            V((NC, R, R), F32),
-            V((NC, R, R), F32),
-            V((R, E), BF16),
+            V((NX, R, W), BF16),
+            V((NX, R, W), BF16),
+            V((NX, R, W), F32),
+            V((NX, R, W), F32),
+            V((NX, R, W), F32),
+            V((R, D), F32),
+            V((2, NX, 1, W), F32),
             V((2, NC, R, R), BF16),
             V((2, NC, R, R), BF16),
             V((2, NC, 1, R), F32),
@@ -664,7 +702,7 @@
         compiler_params=pltpu.CompilerParams(
             collective_id=0, has_side_effects=True, vmem_limit_bytes=40 * 1024 * 1024
         ),
-    )(valid_rows, dest_shard, *[pltpu.with_memory_space_constraint(v, pltpu.HBM) for v in (points, *params)])
+    )(valid_rows, dest_shard[0], *[pltpu.with_memory_space_constraint(v, pltpu.HBM) for v in operands])
 
 
 def solution(mesh):

time: 48 us -> 46.1 us (0.960)
  Pallas kernels: 45.5 us -> 43.7 us
    pallas_call x1, Pallas kernels: 45.5 us -> 43.7 us  [call(): pl.pallas_call(functools.partial(kernel, NY, NZ), out_shape=jax.ShapeDtyp...]
where the time goes in v4:
time: 46.1 us; the launch traced here: 45.7 us
  Pallas kernels  43.7 us (95%)
  between operations  1.3 us (3%)
  local copies, waits for them, and re-layouts  0.66 us (1%)
    pallas_call x1, Pallas kernels, call(): pl.pallas_call(functools.partial(kernel, NY, NZ), out_shape=jax.ShapeDtyp...  43.7 us

profile of v4, /device:TPU:1, one launch (start us, length us, event | category | flops | bytes accessed | tf_op | source)
XLA Modules:
  0.0 45.7 jit_solution(4915881885667270086)
XLA Ops:
  1.3 43.7 %shard_map.118 = bf16[1,128,512]{2,1,0:T(8,128)(2,1)S(1)} custom-call(s32[1,1]{1,0:T(1,128)S(6)} %copy.14.valid_v, s32[1,1]{1,0:T(1,128)} %bitcast.2.dest_v, bf16[1,128,512]{2,1,0:T(8,128)(2,1)} %x_h.1, f32[2,512]{1,0:T(2,128)} %ng_h.1, bf16[2,512,2048]{2,1,0:T(8,128)(2,1)} %wxz_h.1, bf16[2,512,256]{2,1,0:T(8,128)(2,1)} %wbc_h.1, ...), custom_call_target="tpu_custom_call" | custom-call | tf_op jit(solution)/shard_map/pallas_call | solution.py:640
  45.0 0.7 %copy.16 = bf16[1,128,512]{2,1,0:T(8,128)(2,1)} copy(bf16[1,128,512]{2,1,0:T(8,128)(2,1)S(1)} %shard_map.118) | data formatting | bytes 262144

commit v5 on v4

--- a/solution.py
+++ b/solution.py
@@ -445,7 +445,7 @@
     got_l, got_a = send_states(1)
 
     got_m = []
-    for k in (2, 1, 3):
+    for k in (1, 3, 2):
         got_m.append(
             go(mesh_copy(mS, mR.at[k], m_send.at[k], m_recv.at[k], t, curve_peer[2 * k]))
         )

time: 46.1 us -> 45.6 us (0.989)
  no operation moved by 1% of the time
where the time goes in v5:
time: 45.6 us; the launch traced here: 45.5 us
  Pallas kernels  43.5 us (95%)
  between operations  1.3 us (3%)
  local copies, waits for them, and re-layouts  0.66 us (1%)
    pallas_call x1, Pallas kernels, call(): pl.pallas_call(functools.partial(kernel, NY, NZ), out_shape=jax.ShapeDtyp...  43.5 us

profile of v5, /device:TPU:1, one launch (start us, length us, event | category | flops | bytes accessed | tf_op | source)
XLA Modules:
  0.0 45.5 jit_solution(17343698397313389325)
XLA Ops:
  1.3 43.5 %shard_map.118 = bf16[1,128,512]{2,1,0:T(8,128)(2,1)S(1)} custom-call(s32[1,1]{1,0:T(1,128)S(6)} %copy.14.valid_v, s32[1,1]{1,0:T(1,128)} %bitcast.2.dest_v, bf16[1,128,512]{2,1,0:T(8,128)(2,1)} %x_h.1, f32[2,512]{1,0:T(2,128)} %ng_h.1, bf16[2,512,2048]{2,1,0:T(8,128)(2,1)} %wxz_h.1, bf16[2,512,256]{2,1,0:T(8,128)(2,1)} %wbc_h.1, ...), custom_call_target="tpu_custom_call" | custom-call | tf_op jit(solution)/shard_map/pallas_call | solution.py:640
  44.8 0.7 %copy.16 = bf16[1,128,512]{2,1,0:T(8,128)(2,1)} copy(bf16[1,128,512]{2,1,0:T(8,128)(2,1)S(1)} %shard_map.118) | data formatting | bytes 262144

commit v6 on v5

--- a/solution.py
+++ b/solution.py
@@ -604,9 +604,6 @@
     queries = queries_of(nb, 1)
     project_values(nb, 1)
 
-    project_gate(nb, 1)
-    scores = scores_of(keys, queries)
-    running_t, steps_t = running.T, steps.T
     arrive(got)
     entry = jnp.concatenate([rB3[k].astype(F32) for k in range(NZ)], axis=0)
     got, ready = [], None
@@ -618,6 +615,9 @@
         ready = carried_copy(1, k)
     rC[1, c] = (jnp.exp(lpre[c]) * entry + pre[c]).astype(BF16)
     got.append(go(ready))
+    project_gate(nb, 1)
+    scores = scores_of(keys, queries)
+    running_t, steps_t = running.T, steps.T
     inside(1, steps_t, running, running_t, scores, range(NX))
     last = {id(cp) for cp in got}
     for cp in sent:

time: 45.6 us -> 45.6 us (level)
  no operation moved by 1% of the time
where the time goes in v6:
time: 45.6 us; the launch traced here: 45.5 us
  Pallas kernels  43.5 us (95%)
  between operations  1.3 us (3%)
  local copies, waits for them, and re-layouts  0.66 us (1%)
    pallas_call x1, Pallas kernels, call(): pl.pallas_call(functools.partial(kernel, NY, NZ), out_shape=jax.ShapeDtyp...  43.5 us

profile of v6, /device:TPU:1, one launch (start us, length us, event | category | flops | bytes accessed | tf_op | source)
XLA Modules:
  0.0 45.5 jit_solution(13991638327780713178)
XLA Ops:
  1.3 43.5 %shard_map.118 = bf16[1,128,512]{2,1,0:T(8,128)(2,1)S(1)} custom-call(s32[1,1]{1,0:T(1,128)S(6)} %copy.14.valid_v, s32[1,1]{1,0:T(1,128)} %bitcast.2.dest_v, bf16[1,128,512]{2,1,0:T(8,128)(2,1)} %x_h.1, f32[2,512]{1,0:T(2,128)} %ng_h.1, bf16[2,512,2048]{2,1,0:T(8,128)(2,1)} %wxz_h.1, bf16[2,512,256]{2,1,0:T(8,128)(2,1)} %wbc_h.1, ...), custom_call_target="tpu_custom_call" | custom-call | tf_op jit(solution)/shard_map/pallas_call | solution.py:640
  44.8 0.7 %copy.16 = bf16[1,128,512]{2,1,0:T(8,128)(2,1)} copy(bf16[1,128,512]{2,1,0:T(8,128)(2,1)S(1)} %shard_map.118) | data formatting | bytes 262144
